TPU v7x, 32 devices: a whole 2x2x4 slice. The times are simulated.
32 devices in a mesh: head: 4 (over y, x), row: 8 (over z, core).
Axes of the slice: x: 2, y: 2, z: 4, core: 2. Of those that a mesh axis runs over, the one named last changes fastest.
Arguments:
- tokens: bfloat16 [48, 512, 1024], P('row', 'head'), may hold values from -6 to 6
- prev_logits: bfloat16 [48, 16, 512, 512], P('row', 'head'), may hold values from -6 to 6
- segment_ids: int32 [48, 512], P('row'), may hold values from 0 to 3, never falling along the last dimension, each value on 1 to 320 neighbouring positions
- w_qkv: bfloat16 [1024, 3, 1024], P(None, None, 'head'), may hold values from -0.1875 to 0.1875
- b_qv: bfloat16 [2, 1024], P(None, 'head'), may hold values from -3 to 3
- w_out: bfloat16 [1024, 1024], P('head'), may hold values from -1.5 to 1.5
- b_out: bfloat16 [1024], replicated, may hold values from -3 to 3
- ln1_gain: float32 [1024], replicated, may hold values from 0.5 to 1.5
- ln1_shift: float32 [1024], replicated, may hold values from -2 to 2
- w_in: bfloat16 [1024, 4096], P(None, ('head', 'row')), may hold values from -0.1875 to 0.1875
- b_in: bfloat16 [4096], P(('head', 'row')), may hold values from -3 to 3
- w_down: bfloat16 [4096, 1024], P(('head', 'row')), may hold values from -0.1875 to 0.1875
- b_down: bfloat16 [1024], replicated, may hold values from -2 to 2
- ln2_gain: float32 [1024], replicated, may hold values from 0.5 to 1.5
- ln2_shift: float32 [1024], replicated, may hold values from -2 to 2
- out_grad: bfloat16 [48, 512, 1024], P('row', 'head'), may hold values from -6 to 6
- logit_grad: bfloat16 [48, 16, 512, 512], P('row', 'head'), may hold values from -3 to 3
Outputs:
- layer_out: bfloat16 [48, 512, 1024], P('row', 'head')
- raw_logits: bfloat16 [48, 16, 512, 512], P('row', 'head')
- tokens_grad: float32 [48, 512, 1024], P('row', 'head')
- prev_grad: bfloat16 [48, 16, 512, 512], P('row', 'head')
- grad_w_qkv: float32 [1024, 3, 1024], P(None, None, 'head')
- grad_b_qv: float32 [2, 1024], P(None, 'head')
- grad_w_out: float32 [1024, 1024], P('head')
- grad_b_out: float32 [1024], replicated
- grad_ln1_gain: float32 [1024], replicated
- grad_ln1_shift: float32 [1024], replicated
- grad_w_in: float32 [1024, 4096], P(None, ('head', 'row'))
- grad_b_in: float32 [4096], P(('head', 'row'))
- grad_w_down: float32 [4096, 1024], P(('head', 'row'))
- grad_b_down: float32 [1024], replicated
- grad_ln2_gain: float32 [1024], replicated
- grad_ln2_shift: float32 [1024], replicated
Inputs may be any that keep to these rules, and one draw needn't show every extreme that they name: `segment_ids`: in each row of 512 slots the ids never fall and each id covers 1 to 320 slots.
All inputs are finite; a program needn't handle non-finite values.
Results may differ from a plain program's by a relative error of at most 0.015.
Values may be sent and summed in bfloat16 or wider, within the bound.
No kernel may reach another device: no remote copies, remote signals or barrier semaphores. Data moves between devices by JAX's collectives and lax.ppermute only.
A program may use at most 256 MiB of HBM per device.

v0:
```python
import functools

import jax
import jax.numpy as jnp
from jax import lax
from jax.experimental import pallas as pl
from jax.experimental.pallas import tpu as pltpu
from jax.sharding import Mesh
from jax.sharding import PartitionSpec as P

norm_eps = 1e-12
masked_fill = -1000000000.0
head_dim = 64
hidden_block = 512
bias_rows = 16
bf16 = jnp.bfloat16
f32 = jnp.float32


def dot_nn(a, b):
    return lax.dot_general(a, b, (((1,), (0,)), ((), ())), preferred_element_type=f32)


def dot_nt(a, b):
    return lax.dot_general(a, b, (((1,), (1,)), ((), ())), preferred_element_type=f32)


def dot_tn(a, b):
    return lax.dot_general(a, b, (((0,), (0,)), ((), ())), preferred_element_type=f32)


def params(limit_mib=60):
    return pltpu.CompilerParams(
        dimension_semantics=("arbitrary",), vmem_limit_bytes=limit_mib * 1024 * 1024
    )


def cost(flops, nbytes, exps=0):
    return pl.CostEstimate(flops=int(flops), bytes_accessed=int(nbytes), transcendentals=int(exps))


def whole(shape):
    return pl.BlockSpec(shape, lambda *_: (0,) * len(shape))


def by_step(shape, axis=0):
    return pl.BlockSpec(shape, lambda t, *_: tuple(t if d == axis else 0 for d in range(len(shape))))


def norm_parts(values):
    center = jnp.mean(values, axis=-1, keepdims=True)
    offset = values - center
    inverse = lax.rsqrt(jnp.mean(offset * offset, axis=-1, keepdims=True) + norm_eps)
    return offset * inverse, inverse


def norm_back(grad_in, unit_vals, inverse, gain_vec):
    scaled = grad_in * gain_vec
    return inverse * (
        scaled
        - jnp.mean(scaled, axis=-1, keepdims=True)
        - unit_vals * jnp.mean(scaled * unit_vals, axis=-1, keepdims=True)
    )


def lane_halves():
    lane = lax.broadcasted_iota(jnp.int32, (1, 2 * head_dim), 1)
    return lane < head_dim


def attend(me, first, pieces, w_flat, bias_row, seg_row, seg_col, prev, raw_so_far):
    total_rows, heads, slots, _ = prev.shape
    rows, _, width = pieces[0][2].shape
    cols = heads * head_dim
    nh = len({k for k, _, _ in pieces})
    part = slots // nh
    scale = head_dim ** (-0.5)
    np_ = len(pieces)
    places = [(k, off, p.shape[1]) for k, off, p in pieces]
    chained = raw_so_far is not None

    def body(me_ref, *refs):
        toks = refs[:np_]
        w_ref, b_ref, sr_ref, sc_ref, prev_ref = refs[np_ : np_ + 5]
        outs = refs[np_ + 5 + chained :]
        qkv_ref, raw_ref, tok_all, lse_ref = outs[:4]
        ctx_refs = outs[4 : 4 + nh]
        ctx_all = outs[4 + nh]
        mine = me_ref[0]
        for ref, (k, off, size) in zip(toks, places):
            tok_all[0, pl.ds(pl.multiple_of((mine ^ k) * part + off, size), size), :] = ref[0]
        qkv_ref[0] = (dot_nn(tok_all[0], w_ref[...]) + b_ref[...]).astype(bf16)
        low_half = lane_halves()
        keep = [jnp.where(low_half, scale, 0.0).astype(bf16), jnp.where(low_half, 0.0, scale).astype(bf16)]
        lane = lax.broadcasted_iota(jnp.int32, (1, 128), 1)
        same = sc_ref[0] == sr_ref[0]
        lse_tile = jnp.zeros((slots, 128), f32)
        for pair in range(heads // 2):
            span = slice(pair * 128, pair * 128 + 128)
            q_pair = qkv_ref[0, :, span]
            k_pair = qkv_ref[0, :, cols + pair * 128 : cols + pair * 128 + 128]
            v_pair = qkv_ref[0, :, 2 * cols + pair * 128 : 2 * cols + pair * 128 + 128]
            outs = []
            for half in range(2):
                h = 2 * pair + half
                raw = dot_nt(q_pair * keep[half], k_pair) + prev_ref[0, h].astype(f32)
                raw_ref[0, h] = raw.astype(bf16)
                masked = jnp.where(same, raw, masked_fill)
                top = jnp.max(masked, axis=-1, keepdims=True)
                grown = jnp.exp(masked - top)
                total = jnp.sum(grown, axis=-1, keepdims=True)
                probs = (grown * (1.0 / total)).astype(bf16)
                outs.append(dot_nn(probs, v_pair))
                lse_tile = jnp.where(lane == h, top + jnp.log(total), lse_tile)
            ctx_all[:, span] = jnp.where(low_half, outs[0], outs[1]).astype(bf16)
        lse_ref[0] = lse_tile
        for k in range(nh):
            ctx_refs[k][0] = ctx_all[pl.ds(pl.multiple_of((mine ^ k) * part, part), part), :]

    def shifted(shape):
        return pl.BlockSpec(shape, lambda r, *_: (first + r,) + (0,) * (len(shape) - 1))

    return pl.pallas_call(
        body,
        grid_spec=pltpu.PrefetchScalarGridSpec(
            num_scalar_prefetch=1,
            grid=(rows,),
            in_specs=[by_step((1,) + p.shape[1:]) for _, _, p in pieces]
            + [
                whole((width, 3 * cols)),
                whole((1, 3 * cols)),
                shifted((1, 1, slots)),
                shifted((1, slots, 1)),
                shifted((1, heads, slots, slots)),
            ]
            + [pl.BlockSpec(memory_space=pl.ANY)] * chained,
            out_specs=[
                by_step((1, slots, 3 * cols)),
                shifted((1, heads, slots, slots)),
                by_step((1, slots, width)),
                by_step((1, slots, 128)),
            ]
            + [by_step((1, part, cols))] * nh,
            scratch_shapes=[pltpu.VMEM((slots, cols), bf16)],
        ),
        out_shape=[
            jax.ShapeDtypeStruct((rows, slots, 3 * cols), bf16),
            jax.ShapeDtypeStruct((total_rows, heads, slots, slots), bf16),
            jax.ShapeDtypeStruct((rows, slots, width), bf16),
            jax.ShapeDtypeStruct((rows, slots, 128), f32),
        ]
        + [jax.ShapeDtypeStruct((rows, part, cols), bf16)] * nh,
        input_output_aliases={np_ + 6: 1} if chained else {},
        compiler_params=params(),
        cost_estimate=cost(
            2 * rows * slots * cols * (3 * width + 2 * slots), 5 * rows * heads * slots * slots, rows * heads * slots * slots
        ),
        name="attend",
    )(me, *[p for _, _, p in pieces], w_flat, bias_row, seg_row, seg_col, prev, *([raw_so_far] if chained else []))


def attend_back(me, first, tok, ctx_grads, qkv, prev, logit_grad, seg_row, seg_col, lse, w_flat, so_far):
    total_rows, heads, slots, _ = prev.shape
    nh = len(ctx_grads)
    rows, _, width = tok.shape
    part = slots // nh
    cols = heads * head_dim
    half_rows = 3 * cols // 2
    scale = head_dim ** (-0.5)
    chained = so_far is not None

    def body(me_ref, *refs):
        grads = refs[:nh]
        tok_ref, qkv_ref, prev_ref, lg_ref, sr_ref, sc_ref, lse_ref, w_ref = refs[nh : nh + 8]
        rest = refs[nh + 8 :]
        if chained:
            gw_before = rest[1]
            rest = rest[2:]
        pg_ref, gw_ref = rest[:2]
        in_refs = rest[2 : 2 + nh]
        go_all, p_all, dt_all, in_all = rest[2 + nh :]
        mine = me_ref[0]
        for k in range(nh):
            go_all[pl.ds(pl.multiple_of((mine ^ k) * part, part), part), :] = grads[k][0]
        low_half = lane_halves()
        keep_q = [jnp.where(low_half, scale, 0.0).astype(bf16), jnp.where(low_half, 0.0, scale).astype(bf16)]
        keep_g = [jnp.where(low_half, 1.0, 0.0).astype(bf16), jnp.where(low_half, 0.0, 1.0).astype(bf16)]

        same = sc_ref[0] == sr_ref[0]
        for pair in range(heads // 2):
            span = slice(pair * 128, pair * 128 + 128)
            q_pair = qkv_ref[0, :, span]
            g_pair = go_all[:, span]
            k_pair = qkv_ref[0, :, cols + pair * 128 : cols + pair * 128 + 128]
            v_pair = qkv_ref[0, :, 2 * cols + pair * 128 : 2 * cols + pair * 128 + 128]
            for half in range(2):
                h = 2 * pair + half
                raw = dot_nt(q_pair * keep_q[half], k_pair) + prev_ref[0, h].astype(f32)
                probs = jnp.exp(jnp.where(same, raw, masked_fill) - lse_ref[0, :, h : h + 1])
                p_all[h] = probs.astype(bf16)
                pulled = probs * dot_nt(g_pair * keep_g[half], v_pair)
                inner = jnp.sum(pulled, axis=-1, keepdims=True)
                pg_ref[0, h] = (pulled - probs * inner + lg_ref[0, h].astype(f32)).astype(bf16)
        q_t = qkv_ref[0, :, :cols].T
        k_t = qkv_ref[0, :, cols : 2 * cols].T
        g_t = go_all[...].T
        for h in range(heads):
            span = slice(h * head_dim, h * head_dim + head_dim)
            grad_raw = pg_ref[0, h]
            dt_all[h * head_dim : (h + 1) * head_dim, :] = (dot_nt(k_t[span], grad_raw) * scale).astype(bf16)
            dt_all[cols + h * head_dim : cols + (h + 1) * head_dim, :] = (dot_nn(q_t[span], grad_raw) * scale).astype(bf16)
            dt_all[2 * cols + h * head_dim : 2 * cols + (h + 1) * head_dim, :] = dot_nn(g_t[span], p_all[h]).astype(bf16)
        grad_qkv = dt_all[...].T
        in_all[...] = dot_nt(grad_qkv, w_ref[...]).astype(bf16)
        for k in range(nh):
            in_refs[k][0] = in_all[pl.ds(pl.multiple_of((mine ^ k) * part, part), part), :]
        starts = pl.program_id(0) == 0

        @pl.when(starts)
        def _():
            gw_ref[...] = gw_before[...] if chained else jnp.zeros_like(gw_ref)

        gb = dot_nn(jnp.ones((bias_rows, slots), bf16), grad_qkv)
        for half in range(2):
            gw_ref[half, : half_rows, :] += dot_nn(dt_all[half * half_rows : (half + 1) * half_rows, :], tok_ref[0])
            gw_ref[half, half_rows:, : 3 * cols] += gb

    def shifted(shape):
        return pl.BlockSpec(shape, lambda r, *_: (first + r,) + (0,) * (len(shape) - 1))

    sums = [whole((2, half_rows + bias_rows, width))]
    return pl.pallas_call(
        body,
        grid_spec=pltpu.PrefetchScalarGridSpec(
            num_scalar_prefetch=1,
            grid=(rows,),
            in_specs=[by_step((1, part, cols))] * nh
            + [
                by_step((1, slots, width)),
                by_step((1, slots, 3 * cols)),
                shifted((1, heads, slots, slots)),
                shifted((1, heads, slots, slots)),
                shifted((1, 1, slots)),
                shifted((1, slots, 1)),
                by_step((1, slots, 128)),
                whole((width, 3 * cols)),
            ]
            + ([pl.BlockSpec(memory_space=pl.ANY)] + sums if chained else []),
            out_specs=[shifted((1, heads, slots, slots))] + sums + [by_step((1, part, width))] * nh,
            scratch_shapes=[
                pltpu.VMEM((slots, cols), bf16),
                pltpu.VMEM((heads, slots, slots), bf16),
                pltpu.VMEM((3 * cols, slots), bf16),
                pltpu.VMEM((slots, width), bf16),
            ],
        ),
        out_shape=[
            jax.ShapeDtypeStruct((total_rows, heads, slots, slots), bf16),
            jax.ShapeDtypeStruct((2, half_rows + bias_rows, width), f32),
        ]
        + [jax.ShapeDtypeStruct((rows, part, width), bf16)] * nh,
        input_output_aliases={nh + 9: 0} if chained else {},
        compiler_params=params(),
        cost_estimate=cost(
            2 * rows * slots * cols * (6 * width + 5 * slots), 7 * rows * heads * slots * slots, rows * heads * slots * slots
        ),
        name="attend_back",
    )(me, *ctx_grads, tok, qkv, prev, logit_grad, seg_row, seg_col, lse, w_flat, *(so_far if chained else []))


def resident(shape):
    return pl.BlockSpec(shape, lambda *_: (0,) * len(shape), pipeline_mode=pl.Buffered(1))


def fold(values):
    return jnp.sum(values.reshape(values.shape[0] // 8, 8, values.shape[1]), axis=0)


def feed(ctx_pieces, w_out, tokens, vectors, bias_blocks, weights, plan, out_grad):
    count, width = tokens.shape
    nh, nc = len(ctx_pieces), len(ctx_pieces[0])
    cols = ctx_pieces[0][0].shape[1]
    sizes = [p.shape[0] for p in ctx_pieces[0]]
    shard = weights[0].shape[1]
    per_block = hidden_block // shard
    blocks = len(plan)
    hidden = blocks * hidden_block
    strip = 128
    nw = len(weights)
    n_in = nh * nc + 5 + nw

    def body(*refs):
        ctx = refs[: nh * nc]
        wo_ref, tok_ref, vec_ref, bias_ref, og_ref = refs[nh * nc : nh * nc + 5]
        w_refs = refs[nh * nc + 5 : n_in]
        res_out, x_out, gf_out, gres_out, low_out, act_ref, gh_ref, gb_ref, sum_ref = refs[n_in : n_in + 9]
        gc_refs = refs[n_in + 9 : n_in + 9 + nh * nc]
        gwo_ref = refs[n_in + 9 + nh * nc]
        w_all, slope, unit, inv, acc, x_low, res, gf, low, w_sem, out_sem = refs[n_in + 10 + nh * nc :]
        t = pl.program_id(0)

        def sends(which):
            pairs = ((x_low, x_out), (res, res_out), (gf, gf_out), (acc, gres_out), (low, low_out))
            return [pltpu.make_async_copy(*pairs[i], out_sem.at[i]) for i in which]

        def strips(step, init):
            def one(i, carry):
                return step(pl.ds(pl.multiple_of(i * strip, strip), strip), carry)

            return lax.fori_loop(0, count // strip, one, init)

        @pl.when(t == 0)
        def _():
            for block, copies in enumerate(plan):
                for array, low_shard, size, side, to in copies:
                    pltpu.make_async_copy(
                        w_refs[array].at[pl.ds(low_shard, size)], w_all.at[block, side, pl.ds(to, size)], w_sem.at[block]
                    ).start()
            start = 0
            for c in range(nc):
                at = slice(start, start + sizes[c])
                start += sizes[c]
                branch = dot_nn(ctx[c][...], wo_ref[0:cols, :])
                for k in range(1, nh):
                    branch = branch + dot_nn(ctx[k * nc + c][...], wo_ref[k * cols : (k + 1) * cols, :])
                acc[at, :] = branch

            def first_norm(at, carry):
                unit_one, inverse = norm_parts(tok_ref[at, :].astype(f32) + (acc[at, :] + vec_ref[0:1, :]))
                unit[at, :] = unit_one
                inv[at, :] = jnp.broadcast_to(inverse, (strip, 128))
                normed = unit_one * vec_ref[1:2, :] + vec_ref[2:3, :]
                x_low[at, :] = normed.astype(bf16)
                acc[at, :] = normed + vec_ref[3:4, :]
                return carry

            strips(first_norm, 0)
            sends((0,))[0].start()

        @pl.when(t < blocks)
        def _():
            pltpu.make_async_copy(w_all.at[t], w_all.at[t], w_sem.at[t]).wait()
            w_in = w_all[t, 0].reshape(hidden_block, width)
            w_down = w_all[t, 1].reshape(hidden_block, width)
            for m in range(tiles):
                at = slice(m * (count // tiles), (m + 1) * (count // tiles))
                pre = dot_nt(x_low[at, :], w_in) + bias_ref[0]
                below = 0.5 * (1.0 + lax.erf(pre * (0.5**0.5)))
                active = (pre * below).astype(bf16)
                act_ref[at, :] = active
                slope[t, at, :] = (below + pre * (jnp.exp(-0.5 * pre * pre) * 0.3989422804014327)).astype(bf16)
                acc[at, :] += dot_nn(active, w_down)

        @pl.when(t == blocks - 1)
        def _():
            def second_norm(at, carry):
                unit_two, inverse = norm_parts(acc[at, :])
                res[at, :] = (unit_two * vec_ref[4:5, :] + vec_ref[5:6, :]).astype(bf16)
                top = og_ref[at, :].astype(f32)
                grad_two = norm_back(top, unit_two, inverse, vec_ref[4:5, :])
                acc[at, :] = grad_two
                grad_low = grad_two.astype(bf16)
                gf[at, :] = grad_low
                values = (top * unit_two, top, grad_low.astype(f32))
                return tuple(c + fold(v) for c, v in zip(carry, values))

            sums = strips(second_norm, (jnp.zeros((8, width), f32),) * 3)
            for i in range(3):
                sum_ref[i : i + 1, :] = jnp.sum(sums[i], axis=0, keepdims=True)
            for copy in sends((1, 2)):
                copy.start()

        @pl.when(t >= blocks)
        def _():
            w_in = w_all[t - blocks, 0].reshape(hidden_block, width)
            w_down = w_all[t - blocks, 1].reshape(hidden_block, width)
            total = jnp.zeros((8, hidden_block), f32)
            for m in range(tiles):
                at = slice(m * (count // tiles), (m + 1) * (count // tiles))
                grad_hidden = (dot_nt(gf[at, :], w_down) * slope[t - blocks, at, :].astype(f32)).astype(bf16)
                gh_ref[at, :] = grad_hidden
                total = total + fold(grad_hidden.astype(f32))
                acc[at, :] += dot_nn(grad_hidden, w_in)
            gb_ref[0] = jnp.sum(total, axis=0, keepdims=True)

        @pl.when(t == 2 * blocks - 1)
        def _():
            def first_back(at, carry):
                grad_one = acc[at, :]
                unit_one = unit[at, :]
                grad_res = norm_back(grad_one, unit_one, inv[at, 0:1], vec_ref[1:2, :])
                acc[at, :] = grad_res
                grad_low = grad_res.astype(bf16)
                low[at, :] = grad_low
                values = (grad_one * unit_one, grad_one, grad_low.astype(f32))
                return tuple(c + fold(v) for c, v in zip(carry, values))

            sums = strips(first_back, (jnp.zeros((8, width), f32),) * 3)
            for i in range(3):
                sum_ref[3 + i : 4 + i, :] = jnp.sum(sums[i], axis=0, keepdims=True)
            sum_ref[6:8, :] = jnp.zeros((2, width), f32)
            for copy in sends((3, 4)):
                copy.start()
            for k in range(nh):
                grad_ctx = dot_nt(low[...], wo_ref[k * cols : (k + 1) * cols, :]).astype(bf16)
                start = 0
                for c in range(nc):
                    gc_refs[k * nc + c][...] = grad_ctx[start : start + sizes[c]]
                    start += sizes[c]
            for k in range(nh):
                value, start = 0.0, 0
                for c in range(nc):
                    value = value + dot_tn(ctx[k * nc + c][...], low[start : start + sizes[c], :])
                    start += sizes[c]
                gwo_ref[k] = value.astype(bf16)
            for copy in sends(range(5)):
                copy.wait()

    tiles = 1
    anywhere = pl.BlockSpec(memory_space=pl.ANY)
    return pl.pallas_call(
        body,
        grid=(2 * blocks,),
        in_specs=[resident(p.shape) for k in ctx_pieces for p in k]
        + [
            resident(w_out.shape),
            resident((count, width)),
            resident((8, width)),
            pl.BlockSpec((1, 1, hidden_block), lambda t: (jnp.minimum(t, blocks - 1), 0, 0)),
            resident((count, width)),
        ]
        + [anywhere] * nw,
        out_specs=[anywhere] * 5
        + [
            pl.BlockSpec((count, hidden_block), lambda t: (0, jnp.minimum(t, blocks - 1))),
            pl.BlockSpec((count, hidden_block), lambda t: (0, jnp.maximum(t - blocks, 0))),
            pl.BlockSpec((1, 1, hidden_block), lambda t: (jnp.maximum(t - blocks, 0), 0, 0)),
            whole((8, width)),
        ]
        + [whole((n, cols)) for _ in range(nh) for n in sizes]
        + [resident((nh, cols, width))],
        out_shape=[
            jax.ShapeDtypeStruct((count, width), bf16),
            jax.ShapeDtypeStruct((count, width), bf16),
            jax.ShapeDtypeStruct((count, width), bf16),
            jax.ShapeDtypeStruct((count, width), f32),
            jax.ShapeDtypeStruct((count, width), bf16),
            jax.ShapeDtypeStruct((count, hidden), bf16),
            jax.ShapeDtypeStruct((count, hidden), bf16),
            jax.ShapeDtypeStruct((blocks, 1, hidden_block), f32),
            jax.ShapeDtypeStruct((8, width), f32),
        ]
        + [jax.ShapeDtypeStruct((n, cols), bf16) for _ in range(nh) for n in sizes]
        + [jax.ShapeDtypeStruct((nh, cols, width), bf16)],
        scratch_shapes=[
            pltpu.VMEM((blocks, 2, per_block, shard, width), bf16),
            pltpu.VMEM((blocks, count, hidden_block), bf16),
            pltpu.VMEM((count, width), f32),
            pltpu.VMEM((count, 128), f32),
            pltpu.VMEM((count, width), f32),
            pltpu.VMEM((count, width), bf16),
            pltpu.VMEM((count, width), bf16),
            pltpu.VMEM((count, width), bf16),
            pltpu.VMEM((count, width), bf16),
            pltpu.SemaphoreType.DMA((blocks,)),
            pltpu.SemaphoreType.DMA((5,)),
        ],
        compiler_params=params(),
        cost_estimate=cost(4 * count * width * (2 * hidden + width), 4 * hidden * (width + count), 2 * count * hidden),
        name="feed",
    )(*[p for k in ctx_pieces for p in k], w_out, tokens, vectors, bias_blocks, out_grad, *weights)


def weight_grad(left, right, blocks, stride, first, shard, by_place, addend):
    count, width = right.shape
    per_block = hidden_block // shard
    adding = addend is not None
    if by_place:
        spec = pl.BlockSpec((per_block, None, shard, width), lambda t: (0, t, 0, 0))
        shape = (per_block, blocks, shard, width)
    else:
        spec = pl.BlockSpec((None, per_block, shard, width), lambda t: (t, 0, 0, 0))
        shape = (blocks, per_block, shard, width)

    def body(left_ref, right_ref, *refs):
        value = dot_tn(left_ref[...], right_ref[...]).reshape(per_block, shard, width)
        if adding:
            value = value + refs[0][...].astype(f32)
        refs[-1][...] = value.astype(bf16)

    return pl.pallas_call(
        body,
        grid=(blocks,),
        in_specs=[pl.BlockSpec((count, hidden_block), lambda t: (0, first + stride * t)), whole((count, width))]
        + [spec] * adding,
        out_specs=spec,
        out_shape=jax.ShapeDtypeStruct(shape, bf16),
        compiler_params=params(),
        cost_estimate=cost(2 * count * width * hidden_block * blocks, 4 * hidden_block * blocks * (width + count)),
        name="weight_grad",
    )(left, right, *([addend] if adding else []))


def add_turned(pieces):
    def body(*refs):
        refs[-1][...] = sum_of([r[...] for r in refs[:-1]]).T

    rows, width = pieces[0].shape
    return pl.pallas_call(
        body,
        out_shape=jax.ShapeDtypeStruct((width, rows), f32),
        compiler_params=pltpu.CompilerParams(vmem_limit_bytes=32 * 1024 * 1024),
        name="add_turned",
    )(*pieces)


def turn_weights(mine, other, core):
    half, width = mine.shape
    half -= bias_rows
    cols = 2 * half // 3

    def body(core_ref, mine_ref, other_ref, out_ref, all_rows):
        @pl.when(core_ref[0] == 0)
        def _():
            all_rows[0:half, :] = mine_ref[0:half, :].astype(f32)
            all_rows[half : 2 * half, :] = other_ref[0:half, :].astype(f32)

        @pl.when(core_ref[0] != 0)
        def _():
            all_rows[0:half, :] = other_ref[0:half, :].astype(f32)
            all_rows[half : 2 * half, :] = mine_ref[0:half, :].astype(f32)

        for c in range(3):
            out_ref[c] = all_rows[c * cols : (c + 1) * cols, :].T

    return pl.pallas_call(
        body,
        grid_spec=pltpu.PrefetchScalarGridSpec(
            num_scalar_prefetch=1,
            grid=(1,),
            in_specs=[whole(mine.shape)] * 2,
            out_specs=whole((3, width, cols)),
            scratch_shapes=[pltpu.VMEM((2 * half, width), f32)],
        ),
        out_shape=jax.ShapeDtypeStruct((3, width, cols), f32),
        compiler_params=params(),
        name="turn_weights",
    )(core, mine, other)


class Links:
    def __init__(self, head_axes, row_axes, nh, nr):
        self.head_axes, self.row_axes, self.nh, self.nr = head_axes, row_axes, nh, nr
        self.axes = head_axes + row_axes
        self.factored = len(row_axes) == 2

    def swap(self, value, head_bits=0, row_bits=0):
        mask = head_bits * self.nr + row_bits
        return lax.ppermute(value, self.axes, [(i, i ^ mask) for i in range(self.nh * self.nr)])

    def sum_rows(self, value):
        bit = 1
        while bit < self.nr:
            value = value + self.swap(value, 0, bit)
            bit *= 2
        return value

    def sum_heads(self, value):
        bit = 1
        while bit < self.nh:
            value = value + self.swap(value, bit, 0)
            bit *= 2
        return value

    def sum_all(self, value):
        return self.sum_heads(self.sum_rows(value))


def after(value, *others):
    return lax.optimization_barrier((value, *others))[0]


def gather_tokens(links, tokens, chunks, small, early):
    own = [tokens[low : low + size] for low, size in chunks]
    if links.nh != 4:
        return [[(0, 0, t)] + [(k, 0, links.swap(t, k)) for k in range(1, links.nh)] for t in own], None
    result, others, gate = [], None, ()
    for mine in own:
        mine = after(mine, *gate)
        half = mine.shape[1] // 2
        beside, across = links.swap(mine, 1), links.swap(mine, 2)
        if others is None:
            others = exchange(links, small)
            beside, across = hold((beside, across), *early)
        else:
            beside, across = hold((beside, across), *far)
        far = links.swap(across[:, :half], 1), links.swap(beside[:, half:], 2)
        gate = (beside, across)
        result.append([(0, 0, mine), (1, 0, beside), (2, 0, across), (3, 0, far[0]), (3, half, far[1])])
    return result, others


def exchange_first(links, mine):
    return mine, links.swap(mine, 1), links.swap(mine, 2)


def exchange_second(links, mine, beside, across):
    half = mine.shape[0] // 2
    return mine, beside, across, links.swap(across[:half], 1), links.swap(beside[half:], 2)


def exchange(links, mine):
    return exchange_second(links, *exchange_first(links, mine))


def hold(values, *others):
    flat, tree = jax.tree.flatten(values)
    return jax.tree.unflatten(tree, lax.optimization_barrier((*flat, *others))[: len(flat)])


def all_weights(links, in_all, column, beside, across, low, high):
    mine = [in_all, column, beside, across, low, high]
    arrays = mine + [links.swap(a, 0, 1) for a in mine]
    plan = []
    for k in range(4):
        for base in (0, 6):
            copies = [(base, z * 4 + k, 1, 0, z) for z in range(4)]
            if k < 3:
                copies.append((base + 1 + k, 0, 4, 1, 0))
            else:
                copies += [(base + 4, 0, 2, 1, 0), (base + 5, 0, 2, 1, 2)]
            plan.append(copies)
    return arrays, plan


def by_core(first, second, core):
    return jnp.where(core == 0, first, second)


def add_low(a, b):
    return (a.astype(f32) + b.astype(f32)).astype(bf16)


def scatter_first(links, own, beside, across, far):
    half = far.shape[0] // 2
    return own, beside, across, links.swap(far[:half], 1), links.swap(far[half:], 2)


def scatter_second(links, own, beside, across, for_across, for_beside):
    half = for_across.shape[0]
    across = jnp.concatenate([add_low(across[:half], for_across), across[half:]])
    beside = jnp.concatenate([beside[:half], add_low(beside[half:], for_beside)])
    return own, links.swap(beside, 1), links.swap(across, 2)


def scatter_sum(own, beside, across):
    return own.astype(f32) + beside.astype(f32) + across.astype(f32)


def scatter_places(links, total):
    here = lax.axis_index("z")
    pieces = [lax.dynamic_index_in_dim(total, here ^ k, keepdims=False) for k in range(4)]
    return [pieces[0]] + [links.swap(pieces[k], 0, 2 * k) for k in range(1, 4)]


def sum_of(pieces):
    total = pieces[0].astype(f32)
    for piece in pieces[1:]:
        total = total + piece.astype(f32)
    return total


def core_half(links, value, axis):
    core = lax.axis_index("core")
    size = value.shape[axis] // 2
    keep = lax.dynamic_slice_in_dim(value, core * size, size, axis)
    give = lax.dynamic_slice_in_dim(value, (1 - core) * size, size, axis)
    return keep.astype(f32) + links.swap(give.astype(bf16), 0, 1).astype(f32)


def per_device(
    links,
    tokens,
    prev_logits,
    segment_ids,
    w_qkv,
    b_qv,
    w_out,
    b_out,
    ln1_gain,
    ln1_shift,
    w_in,
    b_in,
    w_down,
    b_down,
    ln2_gain,
    ln2_shift,
    out_grad,
    logit_grad,
):
    rows, part, width = tokens.shape
    heads = prev_logits.shape[1]
    cols = heads * head_dim
    shard = w_in.shape[1]
    count = rows * part
    nh, nr = links.nh, links.nr
    me = lax.axis_index(links.head_axes).astype(jnp.int32).reshape(1)
    place = lax.axis_index(links.axes)
    chunks = [(0, rows // 2), (rows // 2, rows - rows // 2)]

    bias_qv = b_qv.astype(f32)
    bias_row = jnp.concatenate([bias_qv[0], jnp.zeros_like(bias_qv[0]), bias_qv[1]])[None]
    w_flat = w_qkv.reshape(width, 3 * cols)
    seg_row = segment_ids[:, None, :]
    seg_col = segment_ids[:, :, None]
    shards = nh * nr
    mine = lax.broadcasted_iota(jnp.int32, (shards, 1), 0) == place
    bias_all = links.sum_all(jnp.where(mine, b_in.astype(f32)[None], 0.0))
    core = lax.axis_index("core") if links.factored else 0
    if links.factored:
        here_h = lax.axis_index(links.head_axes)
        order = jnp.stack(
            [(here_h ^ k) * nr + z * 2 + (core ^ c) for k in range(4) for c in range(2) for z in range(4)]
        )
        bias_blocks = bias_all[order].reshape(-1, 1, hidden_block)
        column = lax.all_gather(w_down[None], "z", axis=0, tiled=True)
        out_half = lax.dynamic_slice_in_dim(w_out, core * (cols // 2), cols // 2)
        small = jnp.concatenate([w_in.T, out_half])
    else:
        bias_blocks = bias_all.reshape(-1, 1, hidden_block)
        small = None
    blocks = bias_blocks.shape[0]
    vectors = jnp.stack(
        [
            b_out.astype(f32),
            ln1_gain,
            ln1_shift,
            b_down.astype(f32),
            ln2_gain,
            ln2_shift,
            jnp.zeros_like(ln1_gain),
            jnp.zeros_like(ln1_gain),
        ]
    )

    early = (bias_row, w_flat, seg_row, seg_col, vectors, bias_blocks)
    tok_pieces, others = gather_tokens(links, tokens, chunks, small, early)
    if links.factored:
        rows_in = [others[0][:shard], others[1][:shard], others[2][:shard], others[3]]
        in_all = lax.all_gather(
            after(jnp.stack(rows_in), column, *(p for _, _, p in tok_pieces[0][1:3])), "z", axis=0, tiled=True
        )
        arrived = [p for _, _, p in tok_pieces[1][1:3]]
        tok_pieces[0] = hold(tok_pieces[0], *arrived)
        tok_pieces[0] = [(k, off, p) for (k, off, _), (_, _, p) in zip(tok_pieces[1], tok_pieces[0])]
        weight_pieces = exchange_first(links, after(column, *arrived))

    raw_logits, saved, ctx_pieces = None, [], [[] for _ in range(nh)]
    for c, ((low, size), pieces) in enumerate(zip(chunks, tok_pieces)):
        if c and links.factored:
            weight_pieces = hold(weight_pieces, raw_logits_gate)
            weight_pieces = exchange_second(links, *weight_pieces)
            near = weight_pieces[1:3] + tuple(p[0] for p in ctx_pieces)
            pieces = [(k, off, after(p, *near) if k == 3 else p) for k, off, p in pieces]
        qkv, raw_logits, tok_all, lse, *ctx = attend(
            me, low, pieces, w_flat, bias_row, seg_row, seg_col, prev_logits, raw_logits
        )
        raw_logits_gate = ctx[0]
        saved.append((qkv, tok_all, lse))
        if c and links.factored:
            ctx = hold(ctx, *(p[0] for p in ctx_pieces))
        for k in range(nh):
            piece = links.swap(ctx[k], k) if k else ctx[k]
            ctx_pieces[k].append(piece.reshape(size * part, cols))
    if links.factored:
        weights, plan = all_weights(links, *hold([in_all, *weight_pieces], raw_logits_gate))
        rows_out = jnp.stack([others[0][shard:], others[1][shard:], others[2][shard:], others[4]])
        rows_out = after(rows_out, raw_logits_gate)
        theirs = links.swap(rows_out, 0, 1)
        w_out_all = jnp.stack([by_core(rows_out, theirs, core), by_core(theirs, rows_out, core)], axis=1)
        w_out_all = w_out_all.reshape(nh * cols, width)
    else:
        weights = [lax.all_gather(a[None], links.axes, axis=0, tiled=True) for a in (w_in.T, w_down)]
        per_block = hidden_block // shard
        plan = [[(side, t * per_block, per_block, side, 0) for side in range(2)] for t in range(blocks)]
        w_out_all = jnp.concatenate([w_out] + [links.swap(w_out, k) for k in range(1, nh)])
    layer_out, x_low, grad_ffn, grad_res, grad_low, active, grad_hidden, gb_in, norm_sums, *rest = feed(
        ctx_pieces,
        w_out_all,
        tokens.reshape(count, width),
        vectors,
        bias_blocks,
        weights,
        plan,
        out_grad.reshape(count, width),
    )
    ctx_grad, gwo = rest[:-1], rest[-1]
    nc = len(chunks)

    def send_ctx(c, *others):
        pieces = hold([ctx_grad[k * nc + c] for k in range(nh)], *others)
        return [(links.swap(p, k) if k else p).reshape(chunks[c][1], part, cols) for k, p in enumerate(pieces)]

    gb_in = gb_in.reshape(shards, shard)
    if links.factored:
        seq = jnp.arange(shards)
        gb_in = gb_in[((seq // nr) ^ here_h) * 8 + ((seq % 2) ^ core) * 4 + (seq % nr) // 2]
    sums = jnp.concatenate([norm_sums[:6], gb_in.reshape(-1, width)])
    ctx_grads = [send_ctx(0)]
    if links.factored:

        def core_swap(g):
            return links.swap(g.reshape(-1, shard, width), 0, 1).reshape(g.shape)

        half = (blocks // 2, 2)
        down_theirs = weight_grad(active, grad_ffn, *half, 1, shard, False, None)
        in_theirs = weight_grad(after(grad_hidden, down_theirs), x_low, *half, 1, shard, True, None)
        down_swapped, in_swapped = core_swap(down_theirs), core_swap(in_theirs)
        ctx_grads.append(send_ctx(1, in_theirs, *ctx_grads[0]))
        gwo = core_half(links, after(gwo, down_theirs), 1).astype(bf16)
        down_own = weight_grad(after(active, in_theirs), grad_ffn, *half, 0, shard, False, down_swapped)
        gwo = after(gwo, down_own, *ctx_grads[0])
        gwo_parts = [gwo[0]] + [links.swap(gwo[k], k) for k in range(1, nh)]
        down_state = scatter_first(links, *(down_own[k] for k in range(4)))
        in_own = weight_grad(after(grad_hidden, down_own), x_low, *half, 0, shard, True, in_swapped)
        in_sum = lax.psum_scatter(in_own.reshape(-1, shard, width), "z", scatter_dimension=0, tiled=True)
        ctx_grads[0] = hold(ctx_grads[0], in_own, *down_state[3:], *ctx_grads[1])
        down_state = scatter_second(links, *hold(down_state, in_own))
        sums = links.sum_rows(after(sums, in_theirs))
    else:
        ctx_grads.append(send_ctx(1))
        own = [
            weight_grad(left, right, blocks, 1, 0, shard, False, None)
            for left, right in ((grad_hidden, x_low), (active, grad_ffn))
        ]
        own_in, own_down = (
            lax.psum_scatter(g.reshape(-1, shard, width), links.axes, scatter_dimension=0, tiled=True)[0] for g in own
        )
        own_in = own_in.astype(f32).T
        gwo_parts = [gwo[0]] + [links.swap(gwo[k], k) for k in range(1, nh)]
        sums = links.sum_rows(sums)

    so_far, returned = None, []
    for c, (low, size) in enumerate(chunks):
        qkv, tok_all, lse = saved[c]
        if links.factored and c:
            down_state, gwo_parts, sums = hold((down_state, gwo_parts, sums), gw)
            down_parts = scatter_places(links, scatter_sum(*down_state).astype(bf16))
            sums = links.sum_heads(sums)
            gwo_total = sum_of(gwo_parts)
            ctx_grads[c] = hold(ctx_grads[c], gwo_total)
        prev_grad, gw, *input_part = attend_back(
            me, low, tok_all, ctx_grads[c], qkv, prev_logits, logit_grad, seg_row, seg_col, lse, w_flat, so_far
        )
        so_far = (prev_grad, gw)
        if links.factored and c:
            gw = core_half(links, after(gw, in_sum), 0)[0].astype(bf16)
            input_part = hold(input_part, gw, *returned[-1])
        returned.append([input_part[0]] + [links.swap(input_part[k], k) for k in range(1, nh)])
    if links.factored:
        in_sum = after(in_sum, gw)
        in_state = scatter_first(links, *(in_sum[k] for k in range(4)))
        own_in = add_turned(scatter_second(links, *in_state))
        own_down = sum_of(down_parts)
        gwo_total, gw = lax.psum((gwo_total.astype(bf16), gw), "z")
        gwo_other, gw_other = links.swap(gwo_total, 0, 1), links.swap(gw, 0, 1)
        grad_w_out = jnp.concatenate([by_core(gwo_total, gwo_other, core), by_core(gwo_other, gwo_total, core)])
        grad_w_qkv = turn_weights(gw, gw_other, core.astype(jnp.int32).reshape(1)).transpose(1, 0, 2)
        gb = gw[-1].astype(f32)
    else:
        sums = links.sum_heads(sums)
        grad_w_out, gw = lax.psum((sum_of(gwo_parts).astype(bf16), gw.astype(bf16)), links.row_axes)
        grad_w_qkv = gw[:, :-bias_rows].astype(f32).reshape(3 * cols, width).T.reshape(width, 3, cols)
        gb = gw[0, -1].astype(f32)
    parts = []
    for (low, size), pieces in zip(chunks, returned):
        total = grad_res.reshape(rows, part, width)[low : low + size]
        for piece in pieces:
            total = total + piece.astype(f32)
        parts.append(total)
    tokens_grad = jnp.concatenate(parts)
    grad_b_qv = jnp.stack([gb[:cols], gb[2 * cols : 3 * cols]])
    totals = sums
    grad_b_in = lax.dynamic_slice_in_dim(totals[6:].reshape(-1), place * shard, shard)
    return (
        layer_out.reshape(rows, part, width),
        raw_logits,
        tokens_grad,
        prev_grad,
        grad_w_qkv,
        grad_b_qv,
        grad_w_out.astype(f32),
        totals[5],
        totals[3],
        totals[4],
        own_in,
        grad_b_in,
        own_down.astype(f32),
        totals[2],
        totals[0],
        totals[1],
    )


def solution(mesh):
    nh, nr = mesh.shape["head"], mesh.shape["row"]
    if (nh, nr) == (4, 8):
        head, row = ("y", "x"), ("z", "core")
        mesh = Mesh(mesh.devices.reshape(2, 2, 4, 2), head + row)
    else:
        head, row = ("head",), ("row",)
    every = head + row
    placed = (
        P(row, head, None),
        P(row, head, None, None),
        P(row, None),
        P(None, None, head),
        P(None, head),
        P(head, None),
        P(),
        P(),
        P(),
        P(None, every),
        P(every),
        P(every, None),
        P(),
        P(),
        P(),
        P(row, head, None),
        P(row, head, None, None),
    )
    return jax.shard_map(
        functools.partial(per_device, Links(head, row, nh, nr)),
        mesh=mesh,
        in_specs=placed,
        out_specs=(
            P(row, head, None),
            P(row, head, None, None),
            P(row, head, None),
            P(row, head, None, None),
            P(None, None, head),
            P(None, head),
            P(head, None),
            P(),
            P(),
            P(),
            P(None, every),
            P(every),
            P(every, None),
            P(),
            P(),
            P(),
        ),
        check_vma=False,
    )
```

profile of v0, /device:TPU:0, one launch (start us, length us, event | category | flops | bytes accessed | tf_op | source)
XLA Modules:
  0.0 463.8 jit_solution(8004466228150320115)
XLA Ops:
  26.5 15.3 %collective-permute-done.5 = f32[32,128]{1,0:T(8,128)S(1)} collective-permute-done((f32[32,128]{1,0:T(8,128)S(1)}, f32[32,128]{1,0:T(8,128)S(1)}, u32[]{:S(2)}, u32[]{:S(2)}) %collective-permute-start.5) | collective-permute-done | bytes 16416 | tf_op jit(solution)/shard_map/ppermute | solution.py:559
  61.5 20.6 %collective-permute-done.7.refs_3_ = bf16[3,64,1024]{2,1,0:T(8,128)(2,1)S(1)} collective-permute-done((bf16[3,64,1024]{2,1,0:T(8,128)(2,1)S(1)}, bf16[3,64,1024]{2,1,0:T(8,128)(2,1)S(1)}, u32[]{:S(2)}, u32[]{:S(2)}) %collective-permute-start.7) | collective-permute-done | bytes 393248 | tf_op jit(solution)/shard_map/ppermute | solution.py:559
  88.4 15.0 %attend.2 = (bf16[3,512,768]{2,1,0:T(8,128)(2,1)}, bf16[6,4,512,512]{3,2,1,0:T(8,128)(2,1)}, bf16[3,512,1024]{2,1,0:T(8,128)(2,1)}, f32[3,512,128]{2,1,0:T(8,128...) custom-call(s32[1]{0:T(128)} %bitcast.me_ref, ...), custom_call_target="tpu_custom_call" | custom-call | flops 3221225472 | bytes 15728640 | tf_op jit(solution)/shard_map/attend/pallas_call | solution.py:123
  116.1 18.7 %collective-permute-done.16 = bf16[3,128,256]{2,1,0:T(8,128)(2,1)S(1)} collective-permute-done((bf16[3,128,256]{2,1,0:T(8,128)(2,1)S(1)}, bf16[3,128,256]{2,1,0:T(8,128)(2,1)S(1)}, u32[]{:S(2)}, u32[]{:S(2)}) %collective-permute-start.16) | collective-permute-done | bytes 196640 | tf_op jit(solution)/shard_map/ppermute | solution.py:559
  136.2 15.0 %attend.3 = (bf16[3,512,768]{2,1,0:T(8,128)(2,1)}, bf16[6,4,512,512]{3,2,1,0:T(8,128)(2,1)}, bf16[3,512,1024]{2,1,0:T(8,128)(2,1)}, f32[3,512,128]{2,1,0:T(8,128...) custom-call(s32[1]{0:T(128)} %bitcast.me_ref, ...), custom_call_target="tpu_custom_call", output_to_operand_aliasing={{1}: (11, {})} | custom-call | flops 3221225472 | bytes 15728640 | tf_op jit(solution)/shard_map/attend/pallas_call | solution.py:123
  152.0 8.0 %collective-permute-done.23 = bf16[128,1024]{1,0:T(8,128)(2,1)S(1)} collective-permute-done((bf16[128,1024]{1,0:T(8,128)(2,1)S(1)}, bf16[128,1024]{1,0:T(8,128)(2,1)S(1)}, u32[]{:S(2)}, u32[]{:S(2)}) %collective-permute-start.23) | collective-permute-done | bytes 262176 | tf_op jit(solution)/shard_map/ppermute | solution.py:559
  163.8 4.2 collective-permute-done.18
  168.1 4.1 collective-permute-done.19
  178.2 53.0 %feed.1 = (bf16[768,1024]{1,0:T(8,128)(2,1)}, bf16[768,1024]{1,0:T(8,128)(2,1)}, bf16[768,1024]{1,0:T(8,128)(2,1)}, f32[768,1024]{1,0:T(8,128)}, bf16[768,1024]{...) custom-call(bf16[384,256]{1,0:T(8,128)(2,1)} %bitcast.197, ...), custom_call_target="tpu_custom_call" | custom-call | flops 28991029248 | bytes 29360128 | tf_op jit(solution)/shard_map/feed/pallas_call | solution.py:421
  231.2 7.3 %weight_grad.4 = bf16[4,4,128,1024]{3,2,1,0:T(8,128)(2,1)} custom-call(bf16[768,4096]{1,0:T(8,128)(2,1)} %get-tuple-element.183.left_ref, bf16[768,1024]{1,0:T(8,128)(2,1)} %get-tuple-element.180.right_ref), custom_call_target="tpu_custom_call" | custom-call | flops 3221225472 | bytes 14680064 | tf_op jit(solution)/shard_map/weight_grad/pallas_call | solution.py:491
  238.6 7.3 %weight_grad.5 = bf16[4,4,128,1024]{3,2,1,0:T(8,128)(2,1)} custom-call(bf16[768,4096]{1,0:T(8,128)(2,1)} %get-tuple-element.184.left_ref, bf16[768,1024]{1,0:T(8,128)(2,1)} %get-tuple-element.182.right_ref), custom_call_target="tpu_custom_call" | custom-call | flops 3221225472 | bytes 14680064 | tf_op jit(solution)/shard_map/weight_grad/pallas_call | solution.py:491
  246.3 8.0 %weight_grad.6 = bf16[4,4,128,1024]{3,2,1,0:T(8,128)(2,1)} custom-call(bf16[768,4096]{1,0:T(8,128)(2,1)} %get-tuple-element.183.left_ref, bf16[768,1024]{1,0:T(8,128)(2,1)} %get-tuple-element.180.right_ref, bf16[4,4,128,1024]{3,2,1,0:T(8,128)(2,1)} %bitcast.76.refs_0_), custom_call_target="tpu_custom_call" | custom-call | flops 3221225472 | bytes 14680064 | tf_op jit(solution)/shard_map/weight_grad/pallas_call | solution.py:491
  254.3 8.1 %weight_grad.7 = bf16[4,4,128,1024]{3,2,1,0:T(8,128)(2,1)} custom-call(bf16[768,4096]{1,0:T(8,128)(2,1)} %get-tuple-element.184.left_ref, bf16[768,1024]{1,0:T(8,128)(2,1)} %get-tuple-element.182.right_ref, bf16[4,4,128,1024]{3,2,1,0:T(8,128)(2,1)} %bitcast.78.refs_0_), custom_call_target="tpu_custom_call" | custom-call | flops 3221225472 | bytes 14680064 | tf_op jit(solution)/shard_map/weight_grad/pallas_call | solution.py:491
  275.6 3.9 collective-permute-done.55
  291.2 7.3 %collective-permute-done.40 = bf16[2,128,1024]{2,1,0:T(8,128)(2,1)S(1)} collective-permute-done((bf16[2,128,1024]{2,1,0:T(8,128)(2,1)S(1)}, bf16[2,128,1024]{2,1,0:T(8,128)(2,1)S(1)}, u32[]{:S(2)}, u32[]{:S(2)}) %collective-permute-start.40) | collective-permute-done | bytes 524320 | tf_op jit(solution)/shard_map/ppermute | solution.py:559
  307.3 22.9 %attend_back.2 = (bf16[6,4,512,512]{3,2,1,0:T(8,128)(2,1)}, f32[2,400,1024]{2,1,0:T(8,128)}, bf16[3,128,1024]{2,1,0:T(8,128)(2,1)}, bf16[3,128,1024]{2,1,0:T(8,1...) custom-call(s32[1]{0:T(128)} %bitcast.me_ref, bf16[3,128,256]{2,1,0:T(8,128)(2,1)} %bitcast.171, ...), custom_call_target="tpu_custom_call" | custom-call | flops 6845104128 | bytes 22020096 | tf_op jit(solution)/shard_map/attend_back/pallas_call | solution.py:232
  330.8 4.6 collective-permute-done.51
  339.3 24.1 %attend_back.3 = (bf16[6,4,512,512]{3,2,1,0:T(8,128)(2,1)}, f32[2,400,1024]{2,1,0:T(8,128)}, bf16[3,128,1024]{2,1,0:T(8,128)(2,1)}, bf16[3,128,1024]{2,1,0:T(8,1...) custom-call(s32[1]{0:T(128)} %bitcast.me_ref, ...), custom_call_target="tpu_custom_call", output_to_operand_aliasing={{0}: (13, {})} | custom-call | flops 6845104128 | bytes 22020096 | tf_op jit(solution)/shard_map/attend_back/pallas_call | solution.py:232
  365.2 5.3 %collective-permute-done.45 = bf16[3,128,1024]{2,1,0:T(8,128)(2,1)} collective-permute-done((bf16[3,128,1024]{2,1,0:T(8,128)(2,1)}, bf16[3,128,1024]{2,1,0:T(8,128)(2,1)}, u32[]{:S(2)}, u32[]{:S(2)}) %collective-permute-start.45) | collective-permute-done | bytes 786464 | tf_op jit(solution)/shard_map/ppermute | solution.py:559
  370.6 3.6 convert_add_fusion.1
  399.4 4.0 collective-permute-done.69
  409.3 23.2 %collective-permute-done.67.refs_2_ = bf16[128,1024]{1,0:T(8,128)(2,1)S(1)} collective-permute-done((bf16[128,1024]{1,0:T(8,128)(2,1)S(1)}, bf16[128,1024]{1,0:T(8,128)(2,1)S(1)}, u32[]{:S(2)}, u32[]{:S(2)}) %collective-permute-start.67) | collective-permute-done | bytes 262176 | tf_op jit(solution)/shard_map/ppermute | solution.py:559
  436.9 10.1 %all-reduce.3.cloned.1.call-done = (bf16[400,1024]{1,0:T(8,128)(2,1)}, bf16[128,1024]{1,0:T(8,128)(2,1)}) async-done(((bf16[400,1024]{1,0:T(8,128)(2,1)}, bf16[128,1024]{1,0:T(8,128)(2,1)}), (bf16[400,1024]{1,0:T(8,128)(2,1)}, bf16[128,1024]{1,0:T(8,128)(2,1)})) %all-reduce.3.cloned.1.call-update) | async-done | bytes 1081360 | tf_op jit(solution)/shard_map/psum | solution.py:865
  452.9 4.1 turn_weights.1
  (339 shorter events, 151.3 us)
Async XLA Ops:
  7.2 47.8 %all-gather.6.cloned.1.call-start = ((), (), s32[]{:S(2)}) async-start(), calls=%async_computation.3 | async-start | bytes 1310720 | tf_op jit(solution)/shard_map/all_gather | solution.py:726
  9.8 45.2 %collective-permute-start = (bf16[3,128,1024]{2,1,0:T(8,128)(2,1)S(1)}, bf16[3,128,1024]{2,1,0:T(8,128)(2,1)}, u32[]{:S(2)}, u32[]{:S(2)}) collective-permute-start(bf16[3,128,1024]{2,1,0:T(8,128)(2,1)S(1)} %get-tuple-element.135.refs_0_), channel_id=1, source_target_pairs={{0,8},{1,9},{2,10},{3,11},{4,12},{5,13},{6,14},{7,15},{8,0},{9,1},... | collective-permute-start | bytes 2359304 | tf_op jit(solution)/shard_map/ppermute | solution.py:559
  12.7 42.3 %collective-permute-start.1 = (bf16[3,128,1024]{2,1,0:T(8,128)(2,1)S(1)}, bf16[3,128,1024]{2,1,0:T(8,128)(2,1)}, u32[]{:S(2)}, u32[]{:S(2)}) collective-permute-start(bf16[3,128,1024]{2,1,0:T(8,128)(2,1)S(1)} %get-tuple-element.135.refs_0_), channel_id=1, source_target_pairs={{0,16},{1,17},{2,18},{3,19},{4,20},{5,21},{6,22},{7,23},{8,24},{9,... | collective-permute-start | bytes 2359304 | tf_op jit(solution)/shard_map/ppermute | solution.py:559
  15.4 28.4 %collective-permute-start.22 = (bf16[256,1024]{1,0:T(8,128)(2,1)}, bf16[256,1024]{1,0:T(8,128)(2,1)S(1)}, u32[]{:S(2)}, u32[]{:S(2)}) collective-permute-start(bf16[256,1024]{1,0:T(8,128)(2,1)} %pad_maximum_fusion.6), channel_id=1, source_target_pairs={{0,16},{1,17},{2,18},{3,19},{4,20},{5,21},{6,22},{7,23},{8,24},{9,... | collective-permute-start | bytes 1572872 | tf_op jit(solution)/shard_map/ppermute | solution.py:559
  15.9 35.1 %collective-permute-start.21 = (bf16[256,1024]{1,0:T(8,128)(2,1)}, bf16[256,1024]{1,0:T(8,128)(2,1)}, u32[]{:S(2)}, u32[]{:S(2)}) collective-permute-start(bf16[256,1024]{1,0:T(8,128)(2,1)} %pad_maximum_fusion.6), channel_id=1, source_target_pairs={{0,8},{1,9},{2,10},{3,11},{4,12},{5,13},{6,14},{7,15},{8,0},{9,1},... | collective-permute-start | bytes 1572872 | tf_op jit(solution)/shard_map/ppermute | solution.py:559
  16.0 135.3 %all-gather.4.cloned.1.call-start = ((), (), s32[]{:S(2)}) async-start(), calls=%async_computation.1 | async-start | bytes 5242880 | tf_op jit(solution)/shard_map/all_gather | solution.py:750
  55.1 308.4 %reduce-scatter.2.cloned.1.call-start = ((), (), s32[]{:S(2)}) async-start(), calls=%async_computation.2 | async-start | bytes 5242880 | tf_op jit(solution)/shard_map/reduce_scatter | solution.py:826
  55.9 27.1 %collective-permute-start.9 = (bf16[3,128,1024]{2,1,0:T(8,128)(2,1)}, bf16[3,128,1024]{2,1,0:T(8,128)(2,1)}, u32[]{:S(2)}, u32[]{:S(2)}) collective-permute-start(bf16[3,128,1024]{2,1,0:T(8,128)(2,1)} %get-tuple-element.132.refs_0_), channel_id=1, source_target_pairs={{0,8},{1,9},{2,10},{3,11},{4,12},{5,13},{6,14},{7,15},{8,0},{9,1},... | collective-permute-start | bytes 2359304 | tf_op jit(solution)/shard_map/ppermute | solution.py:559
  106.4 28.4 %collective-permute-start.17 = (bf16[3,64,1024]{2,1,0:T(8,128)(2,1)S(1)}, bf16[3,64,1024]{2,1,0:T(8,128)(2,1)S(1)}, u32[]{:S(2)}, u32[]{:S(2)}) collective-permute-start(bf16[3,64,1024]{2,1,0:T(8,128)(2,1)S(1)} %slice.190), channel_id=1, source_target_pairs={{0,16},{1,17},{2,18},{3,19},{4,20},{5,21},{6,22},{7,23},{8,24},{9,... | collective-permute-start | bytes 1179656 | tf_op jit(solution)/shard_map/ppermute | solution.py:559
  109.8 41.4 %collective-permute-start.26 = (bf16[2,128,1024]{2,1,0:T(8,128)(2,1)S(1)}, bf16[2,128,1024]{2,1,0:T(8,128)(2,1)S(1)}, u32[]{:S(2)}, u32[]{:S(2)}) collective-permute-start(bf16[2,128,1024]{2,1,0:T(8,128)(2,1)S(1)} %slice.195), channel_id=1, source_target_pairs={{0,8},{1,9},{2,10},{3,11},{4,12},{5,13},{6,14},{7,15},{8,0},{9,1},... | collective-permute-start | bytes 1572872 | tf_op jit(solution)/shard_map/ppermute | solution.py:559
  112.7 38.5 %collective-permute-start.27 = (bf16[2,128,1024]{2,1,0:T(8,128)(2,1)S(1)}, bf16[2,128,1024]{2,1,0:T(8,128)(2,1)}, u32[]{:S(2)}, u32[]{:S(2)}) collective-permute-start(bf16[2,128,1024]{2,1,0:T(8,128)(2,1)S(1)} %slice.196), channel_id=1, source_target_pairs={{0,16},{1,17},{2,18},{3,19},{4,20},{5,21},{6,22},{7,23},{8,24},{9,... | collective-permute-start | bytes 1572872 | tf_op jit(solution)/shard_map/ppermute | solution.py:559
  262.4 184.6 %all-reduce.3.cloned.1.call-start = ((), (), s32[]{:S(2)}) async-start(), calls=%async_computation.4 | async-start | bytes 2162688 | tf_op jit(solution)/shard_map/psum | solution.py:865
  298.8 39.6 %collective-permute-start.48 = (bf16[4,128,1024]{2,1,0:T(8,128)(2,1)S(1)}, bf16[4,128,1024]{2,1,0:T(8,128)(2,1)}, u32[]{:S(2)}, u32[]{:S(2)}) collective-permute-start(bf16[4,128,1024]{2,1,0:T(8,128)(2,1)S(1)} %pad_maximum_fusion.5), channel_id=1, source_target_pairs={{0,16},{1,17},{2,18},{3,19},{4,20},{5,21},{6,22},{7,23},{8,24},{9,... | collective-permute-start | bytes 3145736 | tf_op jit(solution)/shard_map/ppermute | solution.py:559
  301.0 37.4 %collective-permute-start.47 = (bf16[4,128,1024]{2,1,0:T(8,128)(2,1)}, bf16[4,128,1024]{2,1,0:T(8,128)(2,1)}, u32[]{:S(2)}, u32[]{:S(2)}) collective-permute-start(bf16[4,128,1024]{2,1,0:T(8,128)(2,1)} %pad_maximum_fusion.4), channel_id=1, source_target_pairs={{0,8},{1,9},{2,10},{3,11},{4,12},{5,13},{6,14},{7,15},{8,0},{9,1},... | collective-permute-start | bytes 3145736 | tf_op jit(solution)/shard_map/ppermute | solution.py:559
  304.3 31.0 %collective-permute-start.51 = (bf16[128,1024]{1,0:T(8,128)(2,1)}, bf16[128,1024]{1,0:T(8,128)(2,1)S(1)}, u32[]{:S(2)}, u32[]{:S(2)}) collective-permute-start(bf16[128,1024]{1,0:T(8,128)(2,1)} %get-tuple-element.267), channel_id=1, source_target_pairs={{0,16},{1,17},{2,18},{3,19},{4,20},{5,21},{6,22},{7,23},{8,24},{9,... | collective-permute-start | bytes 786440 | tf_op jit(solution)/shard_map/ppermute | solution.py:559
  305.6 30.5 %collective-permute-start.52 = (bf16[128,1024]{1,0:T(8,128)(2,1)S(1)}, bf16[128,1024]{1,0:T(8,128)(2,1)S(1)}, u32[]{:S(2)}, u32[]{:S(2)}) collective-permute-start(bf16[128,1024]{1,0:T(8,128)(2,1)S(1)} %get-tuple-element.266), channel_id=1, source_target_pairs={{0,24},{1,25},{2,26},{3,27},{4,28},{5,29},{6,30},{7,31},{8,16},{9,... | collective-permute-start | bytes 786440 | tf_op jit(solution)/shard_map/ppermute | solution.py:559
  330.3 35.0 %collective-permute-start.44 = (bf16[3,128,1024]{2,1,0:T(8,128)(2,1)}, bf16[3,128,1024]{2,1,0:T(8,128)(2,1)}, u32[]{:S(2)}, u32[]{:S(2)}) collective-permute-start(bf16[3,128,1024]{2,1,0:T(8,128)(2,1)} %get-tuple-element.201), channel_id=1, source_target_pairs={{0,8},{1,9},{2,10},{3,11},{4,12},{5,13},{6,14},{7,15},{8,0},{9,1},... | collective-permute-start | bytes 2359304 | tf_op jit(solution)/shard_map/ppermute | solution.py:559
  335.4 35.2 %collective-permute-start.45 = (bf16[3,128,1024]{2,1,0:T(8,128)(2,1)}, bf16[3,128,1024]{2,1,0:T(8,128)(2,1)}, u32[]{:S(2)}, u32[]{:S(2)}) collective-permute-start(bf16[3,128,1024]{2,1,0:T(8,128)(2,1)} %get-tuple-element.202), channel_id=1, source_target_pairs={{0,16},{1,17},{2,18},{3,19},{4,20},{5,21},{6,22},{7,23},{8,24},{9,... | collective-permute-start | bytes 2359304 | tf_op jit(solution)/shard_map/ppermute | solution.py:559
  336.1 34.5 %collective-permute-start.46 = (bf16[3,128,1024]{2,1,0:T(8,128)(2,1)}, bf16[3,128,1024]{2,1,0:T(8,128)(2,1)}, u32[]{:S(2)}, u32[]{:S(2)}) collective-permute-start(bf16[3,128,1024]{2,1,0:T(8,128)(2,1)} %get-tuple-element.203), channel_id=1, source_target_pairs={{0,24},{1,25},{2,26},{3,27},{4,28},{5,29},{6,30},{7,31},{8,16},{9,... | collective-permute-start | bytes 2359304 | tf_op jit(solution)/shard_map/ppermute | solution.py:559
  392.3 41.1 %collective-permute-start.57 = (bf16[3,128,1024]{2,1,0:T(8,128)(2,1)}, bf16[3,128,1024]{2,1,0:T(8,128)(2,1)S(1)}, u32[]{:S(2)}, u32[]{:S(2)}) collective-permute-start(bf16[3,128,1024]{2,1,0:T(8,128)(2,1)} %get-tuple-element.235), channel_id=1, source_target_pairs={{0,8},{1,9},{2,10},{3,11},{4,12},{5,13},{6,14},{7,15},{8,0},{9,1},... | collective-permute-start | bytes 2359304 | tf_op jit(solution)/shard_map/ppermute | solution.py:559
  394.9 38.6 %collective-permute-start.58 = (bf16[3,128,1024]{2,1,0:T(8,128)(2,1)}, bf16[3,128,1024]{2,1,0:T(8,128)(2,1)S(1)}, u32[]{:S(2)}, u32[]{:S(2)}) collective-permute-start(bf16[3,128,1024]{2,1,0:T(8,128)(2,1)} %get-tuple-element.236), channel_id=1, source_target_pairs={{0,16},{1,17},{2,18},{3,19},{4,20},{5,21},{6,22},{7,23},{8,24},{9,... | collective-permute-start | bytes 2359304 | tf_op jit(solution)/shard_map/ppermute | solution.py:559
  396.0 37.4 %collective-permute-start.59 = (bf16[3,128,1024]{2,1,0:T(8,128)(2,1)}, bf16[3,128,1024]{2,1,0:T(8,128)(2,1)S(1)}, u32[]{:S(2)}, u32[]{:S(2)}) collective-permute-start(bf16[3,128,1024]{2,1,0:T(8,128)(2,1)} %get-tuple-element.237), channel_id=1, source_target_pairs={{0,24},{1,25},{2,26},{3,27},{4,28},{5,29},{6,30},{7,31},{8,16},{9,... | collective-permute-start | bytes 2359304 | tf_op jit(solution)/shard_map/ppermute | solution.py:559
  403.4 29.1 %collective-permute-start.67 = (bf16[128,1024]{1,0:T(8,128)(2,1)S(1)}, bf16[128,1024]{1,0:T(8,128)(2,1)S(1)}, u32[]{:S(2)}, u32[]{:S(2)}) collective-permute-start(bf16[128,1024]{1,0:T(8,128)(2,1)S(1)} %pad_maximum_fusion.8), channel_id=1, source_target_pairs={{0,16},{1,17},{2,18},{3,19},{4,20},{5,21},{6,22},{7,23},{8,24},{9,... | collective-permute-start | bytes 786440 | tf_op jit(solution)/shard_map/ppermute | solution.py:559
  403.4 29.1 %collective-permute-start.65 = (bf16[128,1024]{1,0:T(8,128)(2,1)S(1)}, bf16[128,1024]{1,0:T(8,128)(2,1)S(1)}, u32[]{:S(2)}, u32[]{:S(2)}) collective-permute-start(bf16[128,1024]{1,0:T(8,128)(2,1)S(1)} %pad_maximum_fusion.7), channel_id=1, source_target_pairs={{0,8},{1,9},{2,10},{3,11},{4,12},{5,13},{6,14},{7,15},{8,0},{9,1},... | collective-permute-start | bytes 786440 | tf_op jit(solution)/shard_map/ppermute | solution.py:559
  (107 other events, 1134.9 us)
Sparse Core Ops, SparseCore 0:
  16.1 29.6 all-gather.5
  55.2 80.2 all-gather.3
  262.6 78.4 reduce-scatter.1
  391.3 55.6 all-reduce.2
where the time goes:
time: 467 us; the launch traced here: 464 us
  Pallas kernels  166 us (36%)
  waiting for transfers between devices  144 us (31%)
  starting transfers between devices  76.2 us (16%)
  local copies, waits for them, and re-layouts  38.7 us (8%)
  other arithmetic  24.3 us (5%)
  between operations  14.9 us (3%)
    ppermute x71, waiting for transfers between devices, swap(): lax.ppermute(value, self.axes, [(i, i ^ mask) for i in range(self.nh * se...  134 us
    ppermute x71, starting transfers between devices, swap(): lax.ppermute(value, self.axes, [(i, i ^ mask) for i in range(self.nh * se...  75.7 us
    pallas_call x1, Pallas kernels, feed(): pl.pallas_call(body, grid=(2 * blocks,), in_specs=[resident(p.shape) for...  53 us
    pallas_call x2, Pallas kernels, attend_back(): pl.pallas_call(body, grid_spec=pltpu.PrefetchScalarGridSpec(num_scalar_pr...  47.1 us
    pallas_call x4, Pallas kernels, weight_grad(): pl.pallas_call(body, grid=(blocks,), in_specs=[pl.BlockSpec((count, hidde...  30.7 us
    pallas_call x2, Pallas kernels, attend(): pl.pallas_call(body, grid_spec=pltpu.PrefetchScalarGridSpec(num_scalar_pr...  29.9 us
    psum x1, waiting for transfers between devices, per_device(): gwo_total, gw = lax.psum((gwo_total.astype(bf16), gw), 'z')  10.1 us
  transfers between devices with their start and end apart: 75, of which 26 were waited for; matrix products, arithmetic and copies ran while one was open for 12% of the time, Pallas kernels for 20%

commit v1 on v0

--- a/solution.py
+++ b/solution.py
@@ -159,7 +159,7 @@
     )(me, *[p for _, _, p in pieces], w_flat, bias_row, seg_row, seg_col, prev, *([raw_so_far] if chained else []))
 
 
-def attend_back(me, first, tok, ctx_grads, qkv, prev, logit_grad, seg_row, seg_col, lse, w_flat, so_far):
+def attend_back(me, first, tok, ctx_grads, qkv, prev, logit_grad, seg_row, seg_col, lse, w_flat, start_sums, so_far):
     total_rows, heads, slots, _ = prev.shape
     nh = len(ctx_grads)
     rows, _, width = tok.shape
@@ -171,8 +171,8 @@
 
     def body(me_ref, *refs):
         grads = refs[:nh]
-        tok_ref, qkv_ref, prev_ref, lg_ref, sr_ref, sc_ref, lse_ref, w_ref = refs[nh : nh + 8]
-        rest = refs[nh + 8 :]
+        tok_ref, qkv_ref, prev_ref, lg_ref, sr_ref, sc_ref, lse_ref, w_ref, sums_ref = refs[nh : nh + 9]
+        rest = refs[nh + 9 :]
         if chained:
             gw_before = rest[1]
             rest = rest[2:]
@@ -218,9 +218,15 @@
 
         @pl.when(starts)
         def _():
-            gw_ref[...] = gw_before[...] if chained else jnp.zeros_like(gw_ref)
-
-        gb = dot_nn(jnp.ones((bias_rows, slots), bf16), grad_qkv)
+            if chained:
+                gw_ref[...] = gw_before[...]
+                for half in range(2):
+                    gw_ref[half, half_rows:, :] += sums_ref[...]
+            else:
+                gw_ref[...] = jnp.zeros_like(gw_ref)
+
+        first_row = lax.broadcasted_iota(jnp.int32, (bias_rows, 1), 0) == 0
+        gb = jnp.where(first_row, dot_nn(jnp.ones((bias_rows, slots), bf16), grad_qkv), 0.0)
         for half in range(2):
             gw_ref[half, : half_rows, :] += dot_nn(dt_all[half * half_rows : (half + 1) * half_rows, :], tok_ref[0])
             gw_ref[half, half_rows:, : 3 * cols] += gb
@@ -244,6 +250,7 @@
                 shifted((1, slots, 1)),
                 by_step((1, slots, 128)),
                 whole((width, 3 * cols)),
+                whole((bias_rows, width)),
             ]
             + ([pl.BlockSpec(memory_space=pl.ANY)] + sums if chained else []),
             out_specs=[shifted((1, heads, slots, slots))] + sums + [by_step((1, part, width))] * nh,
@@ -259,13 +266,13 @@
             jax.ShapeDtypeStruct((2, half_rows + bias_rows, width), f32),
         ]
         + [jax.ShapeDtypeStruct((rows, part, width), bf16)] * nh,
-        input_output_aliases={nh + 9: 0} if chained else {},
+        input_output_aliases={nh + 10: 0} if chained else {},
         compiler_params=params(),
         cost_estimate=cost(
             2 * rows * slots * cols * (6 * width + 5 * slots), 7 * rows * heads * slots * slots, rows * heads * slots * slots
         ),
         name="attend_back",
-    )(me, *ctx_grads, tok, qkv, prev, logit_grad, seg_row, seg_col, lse, w_flat, *(so_far if chained else []))
+    )(me, *ctx_grads, tok, qkv, prev, logit_grad, seg_row, seg_col, lse, w_flat, start_sums, *(so_far if chained else []))
 
 
 def resident(shape):
@@ -281,22 +288,24 @@
     nh, nc = len(ctx_pieces), len(ctx_pieces[0])
     cols = ctx_pieces[0][0].shape[1]
     sizes = [p.shape[0] for p in ctx_pieces[0]]
-    shard = weights[0].shape[1]
-    per_block = hidden_block // shard
     blocks = len(plan)
+    per_block = sum(size for _, _, size, side, _ in plan[0] if side == 0)
+    shard = hidden_block // per_block
     hidden = blocks * hidden_block
     strip = 128
     nw = len(weights)
-    n_in = nh * nc + 5 + nw
+    riding = bias_blocks is None
+    n_in = nh * nc + 5 - riding + nw
 
     def body(*refs):
         ctx = refs[: nh * nc]
-        wo_ref, tok_ref, vec_ref, bias_ref, og_ref = refs[nh * nc : nh * nc + 5]
-        w_refs = refs[nh * nc + 5 : n_in]
+        wo_ref, tok_ref, vec_ref, og_ref = refs[nh * nc : nh * nc + 4]
+        bias_ref = None if riding else refs[nh * nc + 4]
+        w_refs = refs[n_in - nw : n_in]
         res_out, x_out, gf_out, gres_out, low_out, act_ref, gh_ref, gb_ref, sum_ref = refs[n_in : n_in + 9]
         gc_refs = refs[n_in + 9 : n_in + 9 + nh * nc]
         gwo_ref = refs[n_in + 9 + nh * nc]
-        w_all, slope, unit, inv, acc, x_low, res, gf, low, w_sem, out_sem = refs[n_in + 10 + nh * nc :]
+        w_all, b_all, slope, unit, inv, acc, x_low, res, gf, low, w_sem, b_sem, out_sem = refs[n_in + 10 + nh * nc :]
         t = pl.program_id(0)
 
         def sends(which):
@@ -313,9 +322,16 @@
         def _():
             for block, copies in enumerate(plan):
                 for array, low_shard, size, side, to in copies:
+                    source = w_refs[array].at[pl.ds(low_shard, size)]
                     pltpu.make_async_copy(
-                        w_refs[array].at[pl.ds(low_shard, size)], w_all.at[block, side, pl.ds(to, size)], w_sem.at[block]
+                        source.at[:, pl.ds(0, shard)], w_all.at[block, side, pl.ds(to, size)], w_sem.at[block]
                     ).start()
+                    if riding and side:
+                        pltpu.make_async_copy(
+                            source.at[:, pl.ds(shard, bias_rows), pl.ds(0, shard)],
+                            b_all.at[block, pl.ds(to, size)],
+                            b_sem.at[block],
+                        ).start()
             start = 0
             for c in range(nc):
                 at = slice(start, start + sizes[c])
@@ -340,11 +356,16 @@
         @pl.when(t < blocks)
         def _():
             pltpu.make_async_copy(w_all.at[t], w_all.at[t], w_sem.at[t]).wait()
+            if riding:
+                pltpu.make_async_copy(b_all.at[t], b_all.at[t], b_sem.at[t]).wait()
+                bias = jnp.concatenate([b_all[t, j, 0:1, :].astype(f32) for j in range(per_block)], axis=1)
+            else:
+                bias = bias_ref[0]
             w_in = w_all[t, 0].reshape(hidden_block, width)
             w_down = w_all[t, 1].reshape(hidden_block, width)
             for m in range(tiles):
                 at = slice(m * (count // tiles), (m + 1) * (count // tiles))
-                pre = dot_nt(x_low[at, :], w_in) + bias_ref[0]
+                pre = dot_nt(x_low[at, :], w_in) + bias
                 below = 0.5 * (1.0 + lax.erf(pre * (0.5**0.5)))
                 active = (pre * below).astype(bf16)
                 act_ref[at, :] = active
@@ -426,9 +447,9 @@
             resident(w_out.shape),
             resident((count, width)),
             resident((8, width)),
-            pl.BlockSpec((1, 1, hidden_block), lambda t: (jnp.minimum(t, blocks - 1), 0, 0)),
             resident((count, width)),
         ]
+        + [pl.BlockSpec((1, 1, hidden_block), lambda t: (jnp.minimum(t, blocks - 1), 0, 0))] * (not riding)
         + [anywhere] * nw,
         out_specs=[anywhere] * 5
         + [
@@ -454,6 +475,7 @@
         + [jax.ShapeDtypeStruct((nh, cols, width), bf16)],
         scratch_shapes=[
             pltpu.VMEM((blocks, 2, per_block, shard, width), bf16),
+            pltpu.VMEM((blocks, per_block, bias_rows, shard), bf16),
             pltpu.VMEM((blocks, count, hidden_block), bf16),
             pltpu.VMEM((count, width), f32),
             pltpu.VMEM((count, 128), f32),
@@ -463,12 +485,13 @@
             pltpu.VMEM((count, width), bf16),
             pltpu.VMEM((count, width), bf16),
             pltpu.SemaphoreType.DMA((blocks,)),
+            pltpu.SemaphoreType.DMA((blocks,)),
             pltpu.SemaphoreType.DMA((5,)),
         ],
         compiler_params=params(),
         cost_estimate=cost(4 * count * width * (2 * hidden + width), 4 * hidden * (width + count), 2 * count * hidden),
         name="feed",
-    )(*[p for k in ctx_pieces for p in k], w_out, tokens, vectors, bias_blocks, out_grad, *weights)
+    )(*[p for k in ctx_pieces for p in k], w_out, tokens, vectors, out_grad, *([] if riding else [bias_blocks]), *weights)
 
 
 def weight_grad(left, right, blocks, stride, first, shard, by_place, addend):
@@ -495,6 +518,7 @@
         + [spec] * adding,
         out_specs=spec,
         out_shape=jax.ShapeDtypeStruct(shape, bf16),
+        input_output_aliases={2: 0} if adding else {},
         compiler_params=params(),
         cost_estimate=cost(2 * count * width * hidden_block * blocks, 4 * hidden_block * blocks * (width + count)),
         name="weight_grad",
@@ -714,22 +738,20 @@
     seg_row = segment_ids[:, None, :]
     seg_col = segment_ids[:, :, None]
     shards = nh * nr
-    mine = lax.broadcasted_iota(jnp.int32, (shards, 1), 0) == place
-    bias_all = links.sum_all(jnp.where(mine, b_in.astype(f32)[None], 0.0))
+    blocks = shards * shard // hidden_block
     core = lax.axis_index("core") if links.factored else 0
     if links.factored:
         here_h = lax.axis_index(links.head_axes)
-        order = jnp.stack(
-            [(here_h ^ k) * nr + z * 2 + (core ^ c) for k in range(4) for c in range(2) for z in range(4)]
-        )
-        bias_blocks = bias_all[order].reshape(-1, 1, hidden_block)
-        column = lax.all_gather(w_down[None], "z", axis=0, tiled=True)
+        bias_blocks = None
+        bias_row_in = jnp.pad(b_in[None], ((0, bias_rows - 1), (0, width - shard)))
+        column = lax.all_gather(jnp.concatenate([w_down, bias_row_in])[None], "z", axis=0, tiled=True)
         out_half = lax.dynamic_slice_in_dim(w_out, core * (cols // 2), cols // 2)
         small = jnp.concatenate([w_in.T, out_half])
     else:
+        mine = lax.broadcasted_iota(jnp.int32, (shards, 1), 0) == place
+        bias_all = links.sum_all(jnp.where(mine, b_in.astype(f32)[None], 0.0))
         bias_blocks = bias_all.reshape(-1, 1, hidden_block)
         small = None
-    blocks = bias_blocks.shape[0]
     vectors = jnp.stack(
         [
             b_out.astype(f32),
@@ -743,7 +765,7 @@
         ]
     )
 
-    early = (bias_row, w_flat, seg_row, seg_col, vectors, bias_blocks)
+    early = (bias_row, w_flat, seg_row, seg_col, vectors)
     tok_pieces, others = gather_tokens(links, tokens, chunks, small, early)
     if links.factored:
         rows_in = [others[0][:shard], others[1][:shard], others[2][:shard], others[3]]
@@ -753,14 +775,15 @@
         arrived = [p for _, _, p in tok_pieces[1][1:3]]
         tok_pieces[0] = hold(tok_pieces[0], *arrived)
         tok_pieces[0] = [(k, off, p) for (k, off, _), (_, _, p) in zip(tok_pieces[1], tok_pieces[0])]
-        weight_pieces = exchange_first(links, after(column, *arrived))
+        tok_pieces[1] = [(k, off, after(p, others[4]) if k in (1, 2) else p) for k, off, p in tok_pieces[1]]
+        weight_pieces = exchange_first(links, after(column, *arrived, others[4]))
 
     raw_logits, saved, ctx_pieces = None, [], [[] for _ in range(nh)]
     for c, ((low, size), pieces) in enumerate(zip(chunks, tok_pieces)):
         if c and links.factored:
             weight_pieces = hold(weight_pieces, raw_logits_gate)
             weight_pieces = exchange_second(links, *weight_pieces)
-            near = weight_pieces[1:3] + tuple(p[0] for p in ctx_pieces)
+            near = weight_pieces[1:3]
             pieces = [(k, off, after(p, *near) if k == 3 else p) for k, off, p in pieces]
         qkv, raw_logits, tok_all, lse, *ctx = attend(
             me, low, pieces, w_flat, bias_row, seg_row, seg_col, prev_logits, raw_logits
@@ -768,14 +791,14 @@
         raw_logits_gate = ctx[0]
         saved.append((qkv, tok_all, lse))
         if c and links.factored:
-            ctx = hold(ctx, *(p[0] for p in ctx_pieces))
+            ctx = hold(ctx, *(p[0] for p in ctx_pieces), *weight_pieces[3:])
         for k in range(nh):
             piece = links.swap(ctx[k], k) if k else ctx[k]
             ctx_pieces[k].append(piece.reshape(size * part, cols))
     if links.factored:
-        weights, plan = all_weights(links, *hold([in_all, *weight_pieces], raw_logits_gate))
+        weights, plan = all_weights(links, *hold([in_all, *weight_pieces], raw_logits_gate, *(p[0] for p in ctx_pieces)))
         rows_out = jnp.stack([others[0][shard:], others[1][shard:], others[2][shard:], others[4]])
-        rows_out = after(rows_out, raw_logits_gate)
+        rows_out = after(rows_out, raw_logits_gate, *(p[0] for p in ctx_pieces))
         theirs = links.swap(rows_out, 0, 1)
         w_out_all = jnp.stack([by_core(rows_out, theirs, core), by_core(theirs, rows_out, core)], axis=1)
         w_out_all = w_out_all.reshape(nh * cols, width)
@@ -807,6 +830,7 @@
         gb_in = gb_in[((seq // nr) ^ here_h) * 8 + ((seq % 2) ^ core) * 4 + (seq % nr) // 2]
     sums = jnp.concatenate([norm_sums[:6], gb_in.reshape(-1, width)])
     ctx_grads = [send_ctx(0)]
+    sums = jnp.pad(sums, ((1, bias_rows - 1 - sums.shape[0]), (0, 0)))
     if links.factored:
 
         def core_swap(g):
@@ -814,19 +838,22 @@
 
         half = (blocks // 2, 2)
         down_theirs = weight_grad(active, grad_ffn, *half, 1, shard, False, None)
-        in_theirs = weight_grad(after(grad_hidden, down_theirs), x_low, *half, 1, shard, True, None)
-        down_swapped, in_swapped = core_swap(down_theirs), core_swap(in_theirs)
-        ctx_grads.append(send_ctx(1, in_theirs, *ctx_grads[0]))
+        sums = sums + links.swap(sums, 1)
+        down_swapped = core_swap(after(down_theirs, sums, *ctx_grads[0]))
+        ctx_grads.append(send_ctx(1, *ctx_grads[0]))
+        in_theirs = weight_grad(after(grad_hidden, down_theirs, sums, *ctx_grads[0]), x_low, *half, 1, shard, True, None)
         gwo = core_half(links, after(gwo, down_theirs), 1).astype(bf16)
-        down_own = weight_grad(after(active, in_theirs), grad_ffn, *half, 0, shard, False, down_swapped)
-        gwo = after(gwo, down_own, *ctx_grads[0])
+        in_swapped = core_swap(after(in_theirs, gwo, *ctx_grads[1]))
+        sums = after(sums, down_theirs)
+        sums = sums + links.swap(sums, 2)
         gwo_parts = [gwo[0]] + [links.swap(gwo[k], k) for k in range(1, nh)]
+        down_own = weight_grad(after(active, in_theirs, sums), grad_ffn, *half, 0, shard, False, down_swapped)
         down_state = scatter_first(links, *(down_own[k] for k in range(4)))
-        in_own = weight_grad(after(grad_hidden, down_own), x_low, *half, 0, shard, True, in_swapped)
+        in_own = weight_grad(after(grad_hidden, down_own, *gwo_parts), x_low, *half, 0, shard, True, in_swapped)
+        in_own = after(in_own, *down_state[3:])
         in_sum = lax.psum_scatter(in_own.reshape(-1, shard, width), "z", scatter_dimension=0, tiled=True)
-        ctx_grads[0] = hold(ctx_grads[0], in_own, *down_state[3:], *ctx_grads[1])
+        ctx_grads[0] = hold(ctx_grads[0], in_own)
         down_state = scatter_second(links, *hold(down_state, in_own))
-        sums = links.sum_rows(after(sums, in_theirs))
     else:
         ctx_grads.append(send_ctx(1))
         own = [
@@ -838,40 +865,43 @@
         )
         own_in = own_in.astype(f32).T
         gwo_parts = [gwo[0]] + [links.swap(gwo[k], k) for k in range(1, nh)]
-        sums = links.sum_rows(sums)
+        sums = links.sum_heads(sums)
 
     so_far, returned = None, []
     for c, (low, size) in enumerate(chunks):
         qkv, tok_all, lse = saved[c]
         if links.factored and c:
-            down_state, gwo_parts, sums = hold((down_state, gwo_parts, sums), gw)
-            down_parts = scatter_places(links, scatter_sum(*down_state).astype(bf16))
-            sums = links.sum_heads(sums)
-            gwo_total = sum_of(gwo_parts)
-            ctx_grads[c] = hold(ctx_grads[c], gwo_total)
+            gwo_total = sum_of(hold(gwo_parts, gw)).astype(bf16)
+            ctx_grads[c] = hold(ctx_grads[c], gwo_total, sums)
         prev_grad, gw, *input_part = attend_back(
-            me, low, tok_all, ctx_grads[c], qkv, prev_logits, logit_grad, seg_row, seg_col, lse, w_flat, so_far
+            me, low, tok_all, ctx_grads[c], qkv, prev_logits, logit_grad, seg_row, seg_col, lse, w_flat, sums, so_far
         )
         so_far = (prev_grad, gw)
-        if links.factored and c:
-            gw = core_half(links, after(gw, in_sum), 0)[0].astype(bf16)
-            input_part = hold(input_part, gw, *returned[-1])
+        if links.factored:
+            if c:
+                gw = core_half(links, after(gw, *returned[0]), 0)[0].astype(bf16)
+                gw, in_sum = hold((gw, in_sum))
+                input_part = hold(input_part, gw)
+            else:
+                input_part = hold(input_part, *down_state[1:])
         returned.append([input_part[0]] + [links.swap(input_part[k], k) for k in range(1, nh)])
     if links.factored:
-        in_sum = after(in_sum, gw)
+        down_state = hold(down_state, *returned[1][1:3])
+        in_sum = after(in_sum, *returned[1])
+        down_parts = scatter_places(links, scatter_sum(*down_state).astype(bf16))
         in_state = scatter_first(links, *(in_sum[k] for k in range(4)))
         own_in = add_turned(scatter_second(links, *in_state))
         own_down = sum_of(down_parts)
-        gwo_total, gw = lax.psum((gwo_total.astype(bf16), gw), "z")
+        gwo_total, gw = lax.psum((gwo_total, gw), "z")
         gwo_other, gw_other = links.swap(gwo_total, 0, 1), links.swap(gw, 0, 1)
         grad_w_out = jnp.concatenate([by_core(gwo_total, gwo_other, core), by_core(gwo_other, gwo_total, core)])
         grad_w_qkv = turn_weights(gw, gw_other, core.astype(jnp.int32).reshape(1)).transpose(1, 0, 2)
-        gb = gw[-1].astype(f32)
+        low_rows = gw[-bias_rows:].astype(f32)
+        returned[0] = hold(returned[0], *returned[1])
     else:
-        sums = links.sum_heads(sums)
         grad_w_out, gw = lax.psum((sum_of(gwo_parts).astype(bf16), gw.astype(bf16)), links.row_axes)
         grad_w_qkv = gw[:, :-bias_rows].astype(f32).reshape(3 * cols, width).T.reshape(width, 3, cols)
-        gb = gw[0, -1].astype(f32)
+        low_rows = gw[0, -bias_rows:].astype(f32)
     parts = []
     for (low, size), pieces in zip(chunks, returned):
         total = grad_res.reshape(rows, part, width)[low : low + size]
@@ -879,9 +909,9 @@
             total = total + piece.astype(f32)
         parts.append(total)
     tokens_grad = jnp.concatenate(parts)
-    grad_b_qv = jnp.stack([gb[:cols], gb[2 * cols : 3 * cols]])
-    totals = sums
-    grad_b_in = lax.dynamic_slice_in_dim(totals[6:].reshape(-1), place * shard, shard)
+    grad_b_qv = jnp.stack([low_rows[0, :cols], low_rows[0, 2 * cols : 3 * cols]])
+    totals = low_rows[1:]
+    grad_b_in = lax.dynamic_slice_in_dim(totals[6 : 6 + shards * shard // width].reshape(-1), place * shard, shard)
     return (
         layer_out.reshape(rows, part, width),
         raw_logits,

time: 467 us -> 469 us (level)
  starting transfers between devices: 76.2 us -> 59.8 us
  Pallas kernels: 166 us -> 176 us
  waiting for transfers between devices: 144 us -> 151 us
    ppermute x71 -> x63, starting transfers between devices: 75.7 us -> 59.7 us  [swap(): lax.ppermute(value, self.axes, [(i, i ^ mask) for i in range(self.nh * se...]
    pallas_call x4, Pallas kernels: 30.7 us -> 41 us  [weight_grad(): pl.pallas_call(body, grid=(blocks,), in_specs=[pl.BlockSpec((count, hidde...]
    ppermute x71 -> x63, waiting for transfers between devices: 134 us -> 143 us  [swap(): lax.ppermute(value, self.axes, [(i, i ^ mask) for i in range(self.nh * se...]
    psum x1, waiting for transfers between devices: 10.1 us -> 3.08 us  [per_device(): gwo_total, gw = lax.psum((gwo_total, gw), 'z')]
    reduce_scatter x1, waiting for transfers between devices: 0.02 us -> 5.18 us  [per_device(): lax.psum_scatter(in_own.reshape(-1, shard, width), 'z', scatter_dimension...]
    unnamed x116 -> x108, local copies, waits for them, and re-layouts: 7.53 us -> 10.1 us
  transfers between devices with their start and end apart: 75 -> 67, of which waited for: 26 -> 28; matrix products, arithmetic and copies ran while one was open for 12% -> 11% of each run, Pallas kernels for 20% -> 24%
where the time goes in v1:
time: 469 us; the launch traced here: 464 us
  Pallas kernels  176 us (38%)
  waiting for transfers between devices  151 us (32%)
  starting transfers between devices  59.8 us (13%)
  local copies, waits for them, and re-layouts  35.6 us (8%)
  other arithmetic  26.3 us (6%)
  between operations  14.9 us (3%)
    ppermute x63, waiting for transfers between devices, swap(): lax.ppermute(value, self.axes, [(i, i ^ mask) for i in range(self.nh * se...  143 us
    ppermute x63, starting transfers between devices, swap(): lax.ppermute(value, self.axes, [(i, i ^ mask) for i in range(self.nh * se...  59.7 us
    pallas_call x1, Pallas kernels, feed(): pl.pallas_call(body, grid=(2 * blocks,), in_specs=[resident(p.shape) for...  52.9 us
    pallas_call x2, Pallas kernels, attend_back(): pl.pallas_call(body, grid_spec=pltpu.PrefetchScalarGridSpec(num_scalar_pr...  47.3 us
    pallas_call x4, Pallas kernels, weight_grad(): pl.pallas_call(body, grid=(blocks,), in_specs=[pl.BlockSpec((count, hidde...  41 us
    pallas_call x2, Pallas kernels, attend(): pl.pallas_call(body, grid_spec=pltpu.PrefetchScalarGridSpec(num_scalar_pr...  30 us
    unnamed x108, local copies, waits for them, and re-layouts  10.1 us
  transfers between devices with their start and end apart: 67, of which 28 were waited for; matrix products, arithmetic and copies ran while one was open for 11% of the time, Pallas kernels for 24%

profile of v1, /device:TPU:0, one launch (start us, length us, event | category | flops | bytes accessed | tf_op | source)
XLA Modules:
  0.0 463.9 jit_solution(7038567334217900417)
XLA Ops:
  17.3 9.8 %collective-permute-done.20 = bf16[256,1024]{1,0:T(8,128)(2,1)S(1)} collective-permute-done((bf16[256,1024]{1,0:T(8,128)(2,1)}, bf16[256,1024]{1,0:T(8,128)(2,1)S(1)}, u32[]{:S(2)}, u32[]{:S(2)}) %collective-permute-start.20) | collective-permute-done | bytes 524320 | tf_op jit(solution)/shard_map/ppermute | solution.py:583
  33.7 13.3 %collective-permute-done.6 = bf16[256,1024]{1,0:T(8,128)(2,1)} collective-permute-done((bf16[256,1024]{1,0:T(8,128)(2,1)}, bf16[256,1024]{1,0:T(8,128)(2,1)}, u32[]{:S(2)}, u32[]{:S(2)}) %collective-permute-start.6) | collective-permute-done | bytes 524320 | tf_op jit(solution)/shard_map/ppermute | solution.py:583
  59.9 20.3 %collective-permute-done.2.refs_3_ = bf16[3,64,1024]{2,1,0:T(8,128)(2,1)S(1)} collective-permute-done((bf16[3,64,1024]{2,1,0:T(8,128)(2,1)S(1)}, bf16[3,64,1024]{2,1,0:T(8,128)(2,1)S(1)}, u32[]{:S(2)}, u32[]{:S(2)}) %collective-permute-start.2) | collective-permute-done | bytes 393248 | tf_op jit(solution)/shard_map/ppermute | solution.py:583
  80.2 3.9 collective-permute-done.3.refs_4_
  96.9 15.0 %attend.2 = (bf16[3,512,768]{2,1,0:T(8,128)(2,1)}, bf16[6,4,512,512]{3,2,1,0:T(8,128)(2,1)}, bf16[3,512,1024]{2,1,0:T(8,128)(2,1)}, f32[3,512,128]{2,1,0:T(8,128...) custom-call(s32[1]{0:T(128)} %bitcast.me_ref, ...), custom_call_target="tpu_custom_call" | custom-call | flops 3221225472 | bytes 15728640 | tf_op jit(solution)/shard_map/attend/pallas_call | solution.py:123
  111.9 5.1 %collective-permute-done.10.refs_15_ = bf16[4,144,1024]{2,1,0:T(8,128)(2,1)} collective-permute-done((bf16[4,144,1024]{2,1,0:T(8,128)(2,1)}, bf16[4,144,1024]{2,1,0:T(8,128)(2,1)}, u32[]{:S(2)}, u32[]{:S(2)}) %collective-permute-start.10) | collective-permute-done | bytes 1179680 | tf_op jit(solution)/shard_map/ppermute | solution.py:583
  127.3 15.0 %attend.3 = (bf16[3,512,768]{2,1,0:T(8,128)(2,1)}, bf16[6,4,512,512]{3,2,1,0:T(8,128)(2,1)}, bf16[3,512,1024]{2,1,0:T(8,128)(2,1)}, f32[3,512,128]{2,1,0:T(8,128...) custom-call(s32[1]{0:T(128)} %bitcast.me_ref, ...), custom_call_target="tpu_custom_call", output_to_operand_aliasing={{1}: (11, {})} | custom-call | flops 3221225472 | bytes 15728640 | tf_op jit(solution)/shard_map/attend/pallas_call | solution.py:123
  148.6 4.3 collective-permute-done.17
  152.9 3.7 collective-permute-done.18
  164.2 52.9 %feed.1 = (bf16[768,1024]{1,0:T(8,128)(2,1)}, bf16[768,1024]{1,0:T(8,128)(2,1)}, bf16[768,1024]{1,0:T(8,128)(2,1)}, f32[768,1024]{1,0:T(8,128)}, bf16[768,1024]{...) custom-call(bf16[384,256]{1,0:T(8,128)(2,1)} %bitcast.163, ...), custom_call_target="tpu_custom_call" | custom-call | flops 28991029248 | bytes 29360128 | tf_op jit(solution)/shard_map/feed/pallas_call | solution.py:442
  217.2 7.4 %weight_grad.4 = bf16[4,4,128,1024]{3,2,1,0:T(8,128)(2,1)} custom-call(bf16[768,4096]{1,0:T(8,128)(2,1)} %get-tuple-element.201.left_ref, bf16[768,1024]{1,0:T(8,128)(2,1)} %get-tuple-element.195.right_ref), custom_call_target="tpu_custom_call" | custom-call | flops 3221225472 | bytes 14680064 | tf_op jit(solution)/shard_map/weight_grad/pallas_call | solution.py:514
  231.0 4.5 collective-permute-done.29
  242.9 7.3 %weight_grad.5 = bf16[4,4,128,1024]{3,2,1,0:T(8,128)(2,1)} custom-call(bf16[768,4096]{1,0:T(8,128)(2,1)} %get-tuple-element.205.left_ref, bf16[768,1024]{1,0:T(8,128)(2,1)} %get-tuple-element.199.right_ref), custom_call_target="tpu_custom_call" | custom-call | flops 3221225472 | bytes 14680064 | tf_op jit(solution)/shard_map/weight_grad/pallas_call | solution.py:514
  260.8 18.1 %weight_grad.6 = bf16[4,4,128,1024]{3,2,1,0:T(8,128)(2,1)} custom-call(bf16[768,4096]{1,0:T(8,128)(2,1)} %get-tuple-element.201.left_ref, bf16[768,1024]{1,0:T(8,128)(2,1)} %get-tuple-element.195.right_ref, bf16[4,4,128,1024]{3,2,1,0:T(8,128)(2,1)} %bitcast.45.refs_0_), custom_call_target="tpu_custom_call", output_to_operand_aliasing={{}: (2, {})} | custom-call | flops 3221225472 | bytes 14680064 | tf_op jit(solution)/shard_map/weight_grad/pallas_call | solution.py:514
  283.0 8.2 %weight_grad.7 = bf16[4,4,128,1024]{3,2,1,0:T(8,128)(2,1)} custom-call(bf16[768,4096]{1,0:T(8,128)(2,1)} %get-tuple-element.205.left_ref, bf16[768,1024]{1,0:T(8,128)(2,1)} %get-tuple-element.199.right_ref, bf16[4,4,128,1024]{3,2,1,0:T(8,128)(2,1)} %bitcast.55.refs_0_), custom_call_target="tpu_custom_call", output_to_operand_aliasing={{}: (2, {})} | custom-call | flops 3221225472 | bytes 14680064 | tf_op jit(solution)/shard_map/weight_grad/pallas_call | solution.py:514
  300.4 23.2 %attend_back.2 = (bf16[6,4,512,512]{3,2,1,0:T(8,128)(2,1)}, f32[2,400,1024]{2,1,0:T(8,128)}, bf16[3,128,1024]{2,1,0:T(8,128)(2,1)}, bf16[3,128,1024]{2,1,0:T(8,1...) custom-call(s32[1]{0:T(128)} %bitcast.me_ref, bf16[3,128,256]{2,1,0:T(8,128)(2,1)} %bitcast.136, ...), custom_call_target="tpu_custom_call" | custom-call | flops 6845104128 | bytes 22020096 | tf_op jit(solution)/shard_map/attend_back/pallas_call | solution.py:238
  329.2 24.1 %attend_back.3 = (bf16[6,4,512,512]{3,2,1,0:T(8,128)(2,1)}, f32[2,400,1024]{2,1,0:T(8,128)}, bf16[3,128,1024]{2,1,0:T(8,128)(2,1)}, bf16[3,128,1024]{2,1,0:T(8,1...) custom-call(s32[1]{0:T(128)} %bitcast.me_ref, ...), custom_call_target="tpu_custom_call", output_to_operand_aliasing={{0}: (14, {})} | custom-call | flops 6845104128 | bytes 22020096 | tf_op jit(solution)/shard_map/attend_back/pallas_call | solution.py:238
  353.4 4.6 collective-permute-done.48
  366.3 5.2 %reduce-scatter.2.cloned.1.call-done = bf16[4,128,1024]{2,1,0:T(8,128)(2,1)} async-done(((bf16[16,128,1024]{2,1,0:T(8,128)(2,1)}), bf16[4,128,1024]{2,1,0:T(8,128)(2,1)}) %reduce-scatter.2.cloned.1.call-update) | async-done | bytes 1048592 | tf_op jit(solution)/shard_map/reduce_scatter | solution.py:854
  377.1 15.1 %collective-permute-done.51 = bf16[3,128,1024]{2,1,0:T(8,128)(2,1)} collective-permute-done((bf16[3,128,1024]{2,1,0:T(8,128)(2,1)}, bf16[3,128,1024]{2,1,0:T(8,128)(2,1)}, u32[]{:S(2)}, u32[]{:S(2)}) %collective-permute-start.51) | collective-permute-done | bytes 786464 | tf_op jit(solution)/shard_map/ppermute | solution.py:583
  392.3 16.9 %collective-permute-done.52 = bf16[3,128,1024]{2,1,0:T(8,128)(2,1)} collective-permute-done((bf16[3,128,1024]{2,1,0:T(8,128)(2,1)}, bf16[3,128,1024]{2,1,0:T(8,128)(2,1)}, u32[]{:S(2)}, u32[]{:S(2)}) %collective-permute-start.52) | collective-permute-done | bytes 786464 | tf_op jit(solution)/shard_map/ppermute | solution.py:583
  426.9 8.7 %collective-permute-done.61 = bf16[128,1024]{1,0:T(8,128)(2,1)S(1)} collective-permute-done((bf16[128,1024]{1,0:T(8,128)(2,1)S(1)}, bf16[128,1024]{1,0:T(8,128)(2,1)S(1)}, u32[]{:S(2)}, u32[]{:S(2)}) %collective-permute-start.61) | collective-permute-done | bytes 262176 | tf_op jit(solution)/shard_map/ppermute | solution.py:583
  435.6 6.2 %collective-permute-done.62 = bf16[128,1024]{1,0:T(8,128)(2,1)S(1)} collective-permute-done((bf16[128,1024]{1,0:T(8,128)(2,1)S(1)}, bf16[128,1024]{1,0:T(8,128)(2,1)S(1)}, u32[]{:S(2)}, u32[]{:S(2)}) %collective-permute-start.62) | collective-permute-done | bytes 262176 | tf_op jit(solution)/shard_map/ppermute | solution.py:583
  452.9 4.1 turn_weights.1
  (300 shorter events, 152.1 us)
Async XLA Ops:
  7.2 46.1 %all-gather.6.cloned.1.call-start = ((), (), s32[]{:S(2)}) async-start(), calls=%async_computation.3 | async-start | bytes 1474560 | tf_op jit(solution)/shard_map/all_gather | solution.py:747
  9.1 135.1 %all-gather.4.cloned.1.call-start = ((), (), s32[]{:S(2)}) async-start(), calls=%async_computation.1 | async-start | bytes 5242880 | tf_op jit(solution)/shard_map/all_gather | solution.py:772
  15.2 38.1 %collective-permute-start = (bf16[3,128,1024]{2,1,0:T(8,128)(2,1)S(1)}, bf16[3,128,1024]{2,1,0:T(8,128)(2,1)}, u32[]{:S(2)}, u32[]{:S(2)}) collective-permute-start(bf16[3,128,1024]{2,1,0:T(8,128)(2,1)S(1)} %get-tuple-element.148.refs_0_), channel_id=1, source_target_pairs={{0,8},{1,9},{2,10},{3,11},{4,12},{5,13},{6,14},{7,15},{8,0},{9,1},... | collective-permute-start | bytes 2359304 | tf_op jit(solution)/shard_map/ppermute | solution.py:583
  16.7 36.6 %collective-permute-start.1 = (bf16[3,128,1024]{2,1,0:T(8,128)(2,1)S(1)}, bf16[3,128,1024]{2,1,0:T(8,128)(2,1)}, u32[]{:S(2)}, u32[]{:S(2)}) collective-permute-start(bf16[3,128,1024]{2,1,0:T(8,128)(2,1)S(1)} %get-tuple-element.148.refs_0_), channel_id=1, source_target_pairs={{0,16},{1,17},{2,18},{3,19},{4,20},{5,21},{6,22},{7,23},{8,24},{9,... | collective-permute-start | bytes 2359304 | tf_op jit(solution)/shard_map/ppermute | solution.py:583
  17.2 29.8 %collective-permute-start.6 = (bf16[256,1024]{1,0:T(8,128)(2,1)}, bf16[256,1024]{1,0:T(8,128)(2,1)}, u32[]{:S(2)}, u32[]{:S(2)}) collective-permute-start(bf16[256,1024]{1,0:T(8,128)(2,1)} %pad_maximum_fusion.6), channel_id=1, source_target_pairs={{0,8},{1,9},{2,10},{3,11},{4,12},{5,13},{6,14},{7,15},{8,0},{9,1},... | collective-permute-start | bytes 1572872 | tf_op jit(solution)/shard_map/ppermute | solution.py:583
  53.3 318.2 %reduce-scatter.2.cloned.1.call-start = ((), (), s32[]{:S(2)}) async-start(), calls=%async_computation.2 | async-start | bytes 5242880 | tf_op jit(solution)/shard_map/reduce_scatter | solution.py:854
  53.4 30.7 %collective-permute-start.4 = (bf16[3,128,1024]{2,1,0:T(8,128)(2,1)}, bf16[3,128,1024]{2,1,0:T(8,128)(2,1)S(1)}, u32[]{:S(2)}, u32[]{:S(2)}) collective-permute-start(bf16[3,128,1024]{2,1,0:T(8,128)(2,1)} %get-tuple-element.145.refs_0_), channel_id=1, source_target_pairs={{0,8},{1,9},{2,10},{3,11},{4,12},{5,13},{6,14},{7,15},{8,0},{9,1},... | collective-permute-start | bytes 2359304 | tf_op jit(solution)/shard_map/ppermute | solution.py:583
  55.0 29.1 %collective-permute-start.5 = (bf16[3,128,1024]{2,1,0:T(8,128)(2,1)}, bf16[3,128,1024]{2,1,0:T(8,128)(2,1)}, u32[]{:S(2)}, u32[]{:S(2)}) collective-permute-start(bf16[3,128,1024]{2,1,0:T(8,128)(2,1)} %get-tuple-element.145.refs_0_), channel_id=1, source_target_pairs={{0,16},{1,17},{2,18},{3,19},{4,20},{5,21},{6,22},{7,23},{8,24},{9,... | collective-permute-start | bytes 2359304 | tf_op jit(solution)/shard_map/ppermute | solution.py:583
  57.9 26.2 %collective-permute-start.3 = (bf16[3,64,1024]{2,1,0:T(8,128)(2,1)S(1)}, bf16[3,64,1024]{2,1,0:T(8,128)(2,1)S(1)}, u32[]{:S(2)}, u32[]{:S(2)}) collective-permute-start(bf16[3,64,1024]{2,1,0:T(8,128)(2,1)S(1)} %slice.193), channel_id=1, source_target_pairs={{0,16},{1,17},{2,18},{3,19},{4,20},{5,21},{6,22},{7,23},{8,24},{9,... | collective-permute-start | bytes 1179656 | tf_op jit(solution)/shard_map/ppermute | solution.py:583
  59.6 27.4 %collective-permute-start.7 = (bf16[128,1024]{1,0:T(8,128)(2,1)S(1)}, bf16[128,1024]{1,0:T(8,128)(2,1)S(1)}, u32[]{:S(2)}, u32[]{:S(2)}) collective-permute-start(bf16[128,1024]{1,0:T(8,128)(2,1)S(1)} %copy-done.26), channel_id=1, source_target_pairs={{0,16},{1,17},{2,18},{3,19},{4,20},{5,21},{6,22},{7,23},{8,24},{9,... | collective-permute-start | bytes 786440 | tf_op jit(solution)/shard_map/ppermute | solution.py:583
  87.7 29.2 %collective-permute-start.10 = (bf16[4,144,1024]{2,1,0:T(8,128)(2,1)}, bf16[4,144,1024]{2,1,0:T(8,128)(2,1)}, u32[]{:S(2)}, u32[]{:S(2)}) collective-permute-start(bf16[4,144,1024]{2,1,0:T(8,128)(2,1)} %bitcast.14.refs_13_), channel_id=1, source_target_pairs={{0,16},{1,17},{2,18},{3,19},{4,20},{5,21},{6,22},{7,23},{8,24},{9,... | collective-permute-start | bytes 3538952 | tf_op jit(solution)/shard_map/ppermute | solution.py:583
  88.2 29.2 %collective-permute-start.9 = (bf16[4,144,1024]{2,1,0:T(8,128)(2,1)}, bf16[4,144,1024]{2,1,0:T(8,128)(2,1)}, u32[]{:S(2)}, u32[]{:S(2)}) collective-permute-start(bf16[4,144,1024]{2,1,0:T(8,128)(2,1)} %bitcast.14.refs_13_), channel_id=1, source_target_pairs={{0,8},{1,9},{2,10},{3,11},{4,12},{5,13},{6,14},{7,15},{8,0},{9,1},... | collective-permute-start | bytes 3538952 | tf_op jit(solution)/shard_map/ppermute | solution.py:583
  93.9 31.4 %collective-permute-start.11 = (bf16[3,64,1024]{2,1,0:T(8,128)(2,1)}, bf16[3,64,1024]{2,1,0:T(8,128)(2,1)S(1)}, u32[]{:S(2)}, u32[]{:S(2)}) collective-permute-start(bf16[3,64,1024]{2,1,0:T(8,128)(2,1)} %slice.197), channel_id=1, source_target_pairs={{0,16},{1,17},{2,18},{3,19},{4,20},{5,21},{6,22},{7,23},{8,24},{9,... | collective-permute-start | bytes 1179656 | tf_op jit(solution)/shard_map/ppermute | solution.py:583
  95.4 30.4 %collective-permute-start.8 = (bf16[3,64,1024]{2,1,0:T(8,128)(2,1)S(1)}, bf16[3,64,1024]{2,1,0:T(8,128)(2,1)S(1)}, u32[]{:S(2)}, u32[]{:S(2)}) collective-permute-start(bf16[3,64,1024]{2,1,0:T(8,128)(2,1)S(1)} %slice.196), channel_id=1, source_target_pairs={{0,8},{1,9},{2,10},{3,11},{4,12},{5,13},{6,14},{7,15},{8,0},{9,1},... | collective-permute-start | bytes 1179656 | tf_op jit(solution)/shard_map/ppermute | solution.py:583
  118.6 25.6 %collective-permute-start.15 = (bf16[2,144,1024]{2,1,0:T(8,128)(2,1)S(1)}, bf16[2,144,1024]{2,1,0:T(8,128)(2,1)}, u32[]{:S(2)}, u32[]{:S(2)}) collective-permute-start(bf16[2,144,1024]{2,1,0:T(8,128)(2,1)S(1)} %slice.198), channel_id=1, source_target_pairs={{0,8},{1,9},{2,10},{3,11},{4,12},{5,13},{6,14},{7,15},{8,0},{9,1},... | collective-permute-start | bytes 1769480 | tf_op jit(solution)/shard_map/ppermute | solution.py:583
  224.7 25.5 %collective-permute-start.35 = (bf16[4,128,1024]{2,1,0:T(8,128)(2,1)S(1)}, bf16[4,128,1024]{2,1,0:T(8,128)(2,1)}, u32[]{:S(2)}, u32[]{:S(2)}) collective-permute-start(bf16[4,128,1024]{2,1,0:T(8,128)(2,1)S(1)} %constant_dynamic-slice_fusion), channel_id=1, source_target_pairs={{0,1},{1,0},{2,3},{3,2},{4,5},{5,4},{6,7},{7,6},{8,9},{9,8},{10,11... | collective-permute-start | bytes 3145736 | tf_op jit(solution)/shard_map/ppermute | solution.py:583
  251.9 31.1 %collective-permute-start.42 = (bf16[16,128,1024]{2,1,0:T(8,128)(2,1)}, bf16[16,128,1024]{2,1,0:T(8,128)(2,1)}, u32[]{:S(2)}, u32[]{:S(2)}) collective-permute-start(bf16[16,128,1024]{2,1,0:T(8,128)(2,1)} %bitcast.127), channel_id=1, source_target_pairs={{0,1},{1,0},{2,3},{3,2},{4,5},{5,4},{6,7},{7,6},{8,9},{9,8},{10,11... | collective-permute-start | bytes 12582920 | tf_op jit(solution)/shard_map/ppermute | solution.py:583
  294.8 151.0 %all-reduce.5.cloned.1.call-start = ((), (), s32[]{:S(2)}) async-start(), calls=%async_computation.4 | async-start | bytes 2162688 | tf_op jit(solution)/shard_map/psum | solution.py:895
  323.7 29.7 %collective-permute-start.47 = (bf16[3,128,1024]{2,1,0:T(8,128)(2,1)}, bf16[3,128,1024]{2,1,0:T(8,128)(2,1)S(1)}, u32[]{:S(2)}, u32[]{:S(2)}) collective-permute-start(bf16[3,128,1024]{2,1,0:T(8,128)(2,1)} %get-tuple-element.232), channel_id=1, source_target_pairs={{0,8},{1,9},{2,10},{3,11},{4,12},{5,13},{6,14},{7,15},{8,0},{9,1},... | collective-permute-start | bytes 2359304 | tf_op jit(solution)/shard_map/ppermute | solution.py:583
  325.2 32.7 %collective-permute-start.48 = (bf16[3,128,1024]{2,1,0:T(8,128)(2,1)}, bf16[3,128,1024]{2,1,0:T(8,128)(2,1)S(1)}, u32[]{:S(2)}, u32[]{:S(2)}) collective-permute-start(bf16[3,128,1024]{2,1,0:T(8,128)(2,1)} %get-tuple-element.233), channel_id=1, source_target_pairs={{0,16},{1,17},{2,18},{3,19},{4,20},{5,21},{6,22},{7,23},{8,24},{9,... | collective-permute-start | bytes 2359304 | tf_op jit(solution)/shard_map/ppermute | solution.py:583
  326.6 31.3 %collective-permute-start.49 = (bf16[3,128,1024]{2,1,0:T(8,128)(2,1)}, bf16[3,128,1024]{2,1,0:T(8,128)(2,1)S(1)}, u32[]{:S(2)}, u32[]{:S(2)}) collective-permute-start(bf16[3,128,1024]{2,1,0:T(8,128)(2,1)} %get-tuple-element.234), channel_id=1, source_target_pairs={{0,24},{1,25},{2,26},{3,27},{4,28},{5,29},{6,30},{7,31},{8,16},{9,... | collective-permute-start | bytes 2359304 | tf_op jit(solution)/shard_map/ppermute | solution.py:583
  373.0 36.2 %collective-permute-start.52 = (bf16[3,128,1024]{2,1,0:T(8,128)(2,1)}, bf16[3,128,1024]{2,1,0:T(8,128)(2,1)}, u32[]{:S(2)}, u32[]{:S(2)}) collective-permute-start(bf16[3,128,1024]{2,1,0:T(8,128)(2,1)} %get-tuple-element.257), channel_id=1, source_target_pairs={{0,16},{1,17},{2,18},{3,19},{4,20},{5,21},{6,22},{7,23},{8,24},{9,... | collective-permute-start | bytes 2359304 | tf_op jit(solution)/shard_map/ppermute | solution.py:583
  374.5 41.9 %collective-permute-start.53 = (bf16[3,128,1024]{2,1,0:T(8,128)(2,1)}, bf16[3,128,1024]{2,1,0:T(8,128)(2,1)}, u32[]{:S(2)}, u32[]{:S(2)}) collective-permute-start(bf16[3,128,1024]{2,1,0:T(8,128)(2,1)} %get-tuple-element.258), channel_id=1, source_target_pairs={{0,24},{1,25},{2,26},{3,27},{4,28},{5,29},{6,30},{7,31},{8,16},{9,... | collective-permute-start | bytes 2359304 | tf_op jit(solution)/shard_map/ppermute | solution.py:583
  415.4 26.4 %collective-permute-start.62 = (bf16[128,1024]{1,0:T(8,128)(2,1)S(1)}, bf16[128,1024]{1,0:T(8,128)(2,1)S(1)}, u32[]{:S(2)}, u32[]{:S(2)}) collective-permute-start(bf16[128,1024]{1,0:T(8,128)(2,1)S(1)} %get-tuple-element.284), channel_id=1, source_target_pairs={{0,6},{1,7},{2,4},{3,5},{4,2},{5,3},{6,0},{7,1},{8,14},{9,15},{10,... | collective-permute-start | bytes 786440 | tf_op jit(solution)/shard_map/ppermute | solution.py:583
  (95 other events, 1027.4 us)
Sparse Core Ops, SparseCore 0:
  10.2 33.1 all-gather.5
  53.5 81.0 all-gather.3
  294.9 76.5 reduce-scatter.1
  377.3 68.5 all-reduce.4

commit v2 on v1

--- a/solution.py
+++ b/solution.py
@@ -68,7 +68,7 @@
     return lane < head_dim
 
 
-def attend(me, first, pieces, w_flat, bias_row, seg_row, seg_col, prev, raw_so_far):
+def attend(me, first, pieces, w_flat, bias_row, seg_row, prev, raw_so_far):
     total_rows, heads, slots, _ = prev.shape
     rows, _, width = pieces[0][2].shape
     cols = heads * head_dim
@@ -81,19 +81,21 @@
 
     def body(me_ref, *refs):
         toks = refs[:np_]
-        w_ref, b_ref, sr_ref, sc_ref, prev_ref = refs[np_ : np_ + 5]
-        outs = refs[np_ + 5 + chained :]
+        w_ref, b_ref, sr_ref, prev_ref = refs[np_ : np_ + 4]
+        outs = refs[np_ + 4 + chained :]
         qkv_ref, raw_ref, tok_all, lse_ref = outs[:4]
         ctx_refs = outs[4 : 4 + nh]
         ctx_all = outs[4 + nh]
         mine = me_ref[0]
         for ref, (k, off, size) in zip(toks, places):
             tok_all[0, pl.ds(pl.multiple_of((mine ^ k) * part + off, size), size), :] = ref[0]
-        qkv_ref[0] = (dot_nn(tok_all[0], w_ref[...]) + b_ref[...]).astype(bf16)
+        for c in range(3):
+            at = slice(c * cols, (c + 1) * cols)
+            qkv_ref[0, :, at] = (dot_nn(tok_all[0], w_ref[c]) + b_ref[:, at]).astype(bf16)
         low_half = lane_halves()
         keep = [jnp.where(low_half, scale, 0.0).astype(bf16), jnp.where(low_half, 0.0, scale).astype(bf16)]
         lane = lax.broadcasted_iota(jnp.int32, (1, 128), 1)
-        same = sc_ref[0] == sr_ref[0]
+        same = jnp.broadcast_to(sr_ref[0], (8, slots)).T[:, 0:1] == sr_ref[0]
         lse_tile = jnp.zeros((slots, 128), f32)
         for pair in range(heads // 2):
             span = slice(pair * 128, pair * 128 + 128)
@@ -127,10 +129,9 @@
             grid=(rows,),
             in_specs=[by_step((1,) + p.shape[1:]) for _, _, p in pieces]
             + [
-                whole((width, 3 * cols)),
+                whole((3, width, cols)),
                 whole((1, 3 * cols)),
                 shifted((1, 1, slots)),
-                shifted((1, slots, 1)),
                 shifted((1, heads, slots, slots)),
             ]
             + [pl.BlockSpec(memory_space=pl.ANY)] * chained,
@@ -150,16 +151,16 @@
             jax.ShapeDtypeStruct((rows, slots, 128), f32),
         ]
         + [jax.ShapeDtypeStruct((rows, part, cols), bf16)] * nh,
-        input_output_aliases={np_ + 6: 1} if chained else {},
+        input_output_aliases={np_ + 5: 1} if chained else {},
         compiler_params=params(),
         cost_estimate=cost(
             2 * rows * slots * cols * (3 * width + 2 * slots), 5 * rows * heads * slots * slots, rows * heads * slots * slots
         ),
         name="attend",
-    )(me, *[p for _, _, p in pieces], w_flat, bias_row, seg_row, seg_col, prev, *([raw_so_far] if chained else []))
-
-
-def attend_back(me, first, tok, ctx_grads, qkv, prev, logit_grad, seg_row, seg_col, lse, w_flat, start_sums, so_far):
+    )(me, *[p for _, _, p in pieces], w_flat, bias_row, seg_row, prev, *([raw_so_far] if chained else []))
+
+
+def attend_back(me, first, tok, ctx_grads, qkv, prev, logit_grad, seg_row, lse, w_flat, start_sums, so_far):
     total_rows, heads, slots, _ = prev.shape
     nh = len(ctx_grads)
     rows, _, width = tok.shape
@@ -171,8 +172,8 @@
 
     def body(me_ref, *refs):
         grads = refs[:nh]
-        tok_ref, qkv_ref, prev_ref, lg_ref, sr_ref, sc_ref, lse_ref, w_ref, sums_ref = refs[nh : nh + 9]
-        rest = refs[nh + 9 :]
+        tok_ref, qkv_ref, prev_ref, lg_ref, sr_ref, lse_ref, w_ref, sums_ref = refs[nh : nh + 8]
+        rest = refs[nh + 8 :]
         if chained:
             gw_before = rest[1]
             rest = rest[2:]
@@ -186,7 +187,7 @@
         keep_q = [jnp.where(low_half, scale, 0.0).astype(bf16), jnp.where(low_half, 0.0, scale).astype(bf16)]
         keep_g = [jnp.where(low_half, 1.0, 0.0).astype(bf16), jnp.where(low_half, 0.0, 1.0).astype(bf16)]
 
-        same = sc_ref[0] == sr_ref[0]
+        same = jnp.broadcast_to(sr_ref[0], (8, slots)).T[:, 0:1] == sr_ref[0]
         for pair in range(heads // 2):
             span = slice(pair * 128, pair * 128 + 128)
             q_pair = qkv_ref[0, :, span]
@@ -211,7 +212,10 @@
             dt_all[cols + h * head_dim : cols + (h + 1) * head_dim, :] = (dot_nn(q_t[span], grad_raw) * scale).astype(bf16)
             dt_all[2 * cols + h * head_dim : 2 * cols + (h + 1) * head_dim, :] = dot_nn(g_t[span], p_all[h]).astype(bf16)
         grad_qkv = dt_all[...].T
-        in_all[...] = dot_nt(grad_qkv, w_ref[...]).astype(bf16)
+        in_part = dot_nt(grad_qkv[:, :cols], w_ref[0])
+        for c in range(1, 3):
+            in_part = in_part + dot_nt(grad_qkv[:, c * cols : (c + 1) * cols], w_ref[c])
+        in_all[...] = in_part.astype(bf16)
         for k in range(nh):
             in_refs[k][0] = in_all[pl.ds(pl.multiple_of((mine ^ k) * part, part), part), :]
         starts = pl.program_id(0) == 0
@@ -247,9 +251,8 @@
                 shifted((1, heads, slots, slots)),
                 shifted((1, heads, slots, slots)),
                 shifted((1, 1, slots)),
-                shifted((1, slots, 1)),
                 by_step((1, slots, 128)),
-                whole((width, 3 * cols)),
+                whole((3, width, cols)),
                 whole((bias_rows, width)),
             ]
             + ([pl.BlockSpec(memory_space=pl.ANY)] + sums if chained else []),
@@ -266,13 +269,13 @@
             jax.ShapeDtypeStruct((2, half_rows + bias_rows, width), f32),
         ]
         + [jax.ShapeDtypeStruct((rows, part, width), bf16)] * nh,
-        input_output_aliases={nh + 10: 0} if chained else {},
+        input_output_aliases={nh + 9: 0} if chained else {},
         compiler_params=params(),
         cost_estimate=cost(
             2 * rows * slots * cols * (6 * width + 5 * slots), 7 * rows * heads * slots * slots, rows * heads * slots * slots
         ),
         name="attend_back",
-    )(me, *ctx_grads, tok, qkv, prev, logit_grad, seg_row, seg_col, lse, w_flat, start_sums, *(so_far if chained else []))
+    )(me, *ctx_grads, tok, qkv, prev, logit_grad, seg_row, lse, w_flat, start_sums, *(so_far if chained else []))
 
 
 def resident(shape):
@@ -734,9 +737,8 @@
 
     bias_qv = b_qv.astype(f32)
     bias_row = jnp.concatenate([bias_qv[0], jnp.zeros_like(bias_qv[0]), bias_qv[1]])[None]
-    w_flat = w_qkv.reshape(width, 3 * cols)
+    w_flat = w_qkv.transpose(1, 0, 2)
     seg_row = segment_ids[:, None, :]
-    seg_col = segment_ids[:, :, None]
     shards = nh * nr
     blocks = shards * shard // hidden_block
     core = lax.axis_index("core") if links.factored else 0
@@ -765,7 +767,7 @@
         ]
     )
 
-    early = (bias_row, w_flat, seg_row, seg_col, vectors)
+    early = (bias_row, vectors)
     tok_pieces, others = gather_tokens(links, tokens, chunks, small, early)
     if links.factored:
         rows_in = [others[0][:shard], others[1][:shard], others[2][:shard], others[3]]
@@ -786,7 +788,7 @@
             near = weight_pieces[1:3]
             pieces = [(k, off, after(p, *near) if k == 3 else p) for k, off, p in pieces]
         qkv, raw_logits, tok_all, lse, *ctx = attend(
-            me, low, pieces, w_flat, bias_row, seg_row, seg_col, prev_logits, raw_logits
+            me, low, pieces, w_flat, bias_row, seg_row, prev_logits, raw_logits
         )
         raw_logits_gate = ctx[0]
         saved.append((qkv, tok_all, lse))
@@ -843,11 +845,11 @@
         ctx_grads.append(send_ctx(1, *ctx_grads[0]))
         in_theirs = weight_grad(after(grad_hidden, down_theirs, sums, *ctx_grads[0]), x_low, *half, 1, shard, True, None)
         gwo = core_half(links, after(gwo, down_theirs), 1).astype(bf16)
-        in_swapped = core_swap(after(in_theirs, gwo, *ctx_grads[1]))
+        in_swapped = core_swap(in_theirs)
         sums = after(sums, down_theirs)
         sums = sums + links.swap(sums, 2)
         gwo_parts = [gwo[0]] + [links.swap(gwo[k], k) for k in range(1, nh)]
-        down_own = weight_grad(after(active, in_theirs, sums), grad_ffn, *half, 0, shard, False, down_swapped)
+        down_own = weight_grad(after(active, in_swapped, sums, gwo, *ctx_grads[1]), grad_ffn, *half, 0, shard, False, down_swapped)
         down_state = scatter_first(links, *(down_own[k] for k in range(4)))
         in_own = weight_grad(after(grad_hidden, down_own, *gwo_parts), x_low, *half, 0, shard, True, in_swapped)
         in_own = after(in_own, *down_state[3:])
@@ -874,7 +876,7 @@
             gwo_total = sum_of(hold(gwo_parts, gw)).astype(bf16)
             ctx_grads[c] = hold(ctx_grads[c], gwo_total, sums)
         prev_grad, gw, *input_part = attend_back(
-            me, low, tok_all, ctx_grads[c], qkv, prev_logits, logit_grad, seg_row, seg_col, lse, w_flat, sums, so_far
+            me, low, tok_all, ctx_grads[c], qkv, prev_logits, logit_grad, seg_row, lse, w_flat, sums, so_far
         )
         so_far = (prev_grad, gw)
         if links.factored:

time: 469 us -> 466 us (level)
  local copies, waits for them, and re-layouts: 35.6 us -> 28.8 us
    unnamed x108 -> x113, local copies, waits for them, and re-layouts: 10.1 us -> 7.12 us
  transfers between devices with their start and end apart: 67 -> 67, of which waited for: 28 -> 30; matrix products, arithmetic and copies ran while one was open for 11% -> 10% of each run, Pallas kernels for 24% -> 24%
where the time goes in v2:
time: 466 us; the launch traced here: 462 us
  Pallas kernels  177 us (38%)
  waiting for transfers between devices  152 us (33%)
  starting transfers between devices  64 us (14%)
  local copies, waits for them, and re-layouts  28.8 us (6%)
  other arithmetic  25.7 us (6%)
  between operations  14.9 us (3%)
    ppermute x63, waiting for transfers between devices, swap(): lax.ppermute(value, self.axes, [(i, i ^ mask) for i in range(self.nh * se...  141 us
    ppermute x63, starting transfers between devices, swap(): lax.ppermute(value, self.axes, [(i, i ^ mask) for i in range(self.nh * se...  63.9 us
    pallas_call x1, Pallas kernels, feed(): pl.pallas_call(body, grid=(2 * blocks,), in_specs=[resident(p.shape) for...  52.9 us
    pallas_call x2, Pallas kernels, attend_back(): pl.pallas_call(body, grid_spec=pltpu.PrefetchScalarGridSpec(num_scalar_pr...  47.8 us
    pallas_call x4, Pallas kernels, weight_grad(): pl.pallas_call(body, grid=(blocks,), in_specs=[pl.BlockSpec((count, hidde...  41.2 us
    pallas_call x2, Pallas kernels, attend(): pl.pallas_call(body, grid_spec=pltpu.PrefetchScalarGridSpec(num_scalar_pr...  29.8 us
  transfers between devices with their start and end apart: 67, of which 30 were waited for; matrix products, arithmetic and copies ran while one was open for 10% of the time, Pallas kernels for 24%

profile of v2, /device:TPU:0, one launch (start us, length us, event | category | flops | bytes accessed | tf_op | source)
XLA Modules:
  0.0 461.8 jit_solution(6864428285656473912)
XLA Ops:
  17.0 10.1 %collective-permute-done.20 = bf16[256,1024]{1,0:T(8,128)(2,1)S(1)} collective-permute-done((bf16[256,1024]{1,0:T(8,128)(2,1)}, bf16[256,1024]{1,0:T(8,128)(2,1)S(1)}, u32[]{:S(2)}, u32[]{:S(2)}) %collective-permute-start.20) | collective-permute-done | bytes 524320 | tf_op jit(solution)/shard_map/ppermute | solution.py:586
  31.3 14.8 %collective-permute-done.6 = bf16[256,1024]{1,0:T(8,128)(2,1)} collective-permute-done((bf16[256,1024]{1,0:T(8,128)(2,1)}, bf16[256,1024]{1,0:T(8,128)(2,1)}, u32[]{:S(2)}, u32[]{:S(2)}) %collective-permute-start.6) | collective-permute-done | bytes 524320 | tf_op jit(solution)/shard_map/ppermute | solution.py:586
  58.7 20.4 %collective-permute-done.2.refs_3_ = bf16[3,64,1024]{2,1,0:T(8,128)(2,1)S(1)} collective-permute-done((bf16[3,64,1024]{2,1,0:T(8,128)(2,1)S(1)}, bf16[3,64,1024]{2,1,0:T(8,128)(2,1)S(1)}, u32[]{:S(2)}, u32[]{:S(2)}) %collective-permute-start.2) | collective-permute-done | bytes 393248 | tf_op jit(solution)/shard_map/ppermute | solution.py:586
  79.2 3.9 collective-permute-done.3.refs_4_
  93.3 14.8 %attend.2 = (bf16[3,512,768]{2,1,0:T(8,128)(2,1)}, bf16[6,4,512,512]{3,2,1,0:T(8,128)(2,1)}, bf16[3,512,1024]{2,1,0:T(8,128)(2,1)}, f32[3,512,128]{2,1,0:T(8,128...) custom-call(s32[1]{0:T(128)} %bitcast.me_ref, ...), custom_call_target="tpu_custom_call" | custom-call | flops 3221225472 | bytes 15728640 | tf_op jit(solution)/shard_map/attend/pallas_call | solution.py:125
  108.1 7.1 %collective-permute-done.10.refs_15_ = bf16[4,144,1024]{2,1,0:T(8,128)(2,1)} collective-permute-done((bf16[4,144,1024]{2,1,0:T(8,128)(2,1)}, bf16[4,144,1024]{2,1,0:T(8,128)(2,1)}, u32[]{:S(2)}, u32[]{:S(2)}) %collective-permute-start.10) | collective-permute-done | bytes 1179680 | tf_op jit(solution)/shard_map/ppermute | solution.py:586
  125.6 15.0 %attend.3 = (bf16[3,512,768]{2,1,0:T(8,128)(2,1)}, bf16[6,4,512,512]{3,2,1,0:T(8,128)(2,1)}, bf16[3,512,1024]{2,1,0:T(8,128)(2,1)}, f32[3,512,128]{2,1,0:T(8,128...) custom-call(s32[1]{0:T(128)} %bitcast.me_ref, ...), custom_call_target="tpu_custom_call", output_to_operand_aliasing={{1}: (10, {})} | custom-call | flops 3221225472 | bytes 15728640 | tf_op jit(solution)/shard_map/attend/pallas_call | solution.py:125
  147.3 4.3 collective-permute-done.17
  152.1 3.3 collective-permute-done.19
  162.1 52.9 %feed.1 = (bf16[768,1024]{1,0:T(8,128)(2,1)}, bf16[768,1024]{1,0:T(8,128)(2,1)}, bf16[768,1024]{1,0:T(8,128)(2,1)}, f32[768,1024]{1,0:T(8,128)}, bf16[768,1024]{...) custom-call(bf16[384,256]{1,0:T(8,128)(2,1)} %bitcast.164, ...), custom_call_target="tpu_custom_call" | custom-call | flops 28991029248 | bytes 29360128 | tf_op jit(solution)/shard_map/feed/pallas_call | solution.py:445
  222.9 7.3 %weight_grad.4 = bf16[4,4,128,1024]{3,2,1,0:T(8,128)(2,1)} custom-call(bf16[768,4096]{1,0:T(8,128)(2,1)} %get-tuple-element.210.left_ref, bf16[768,1024]{1,0:T(8,128)(2,1)} %get-tuple-element.194.right_ref), custom_call_target="tpu_custom_call" | custom-call | flops 3221225472 | bytes 14680064 | tf_op jit(solution)/shard_map/weight_grad/pallas_call | solution.py:517
  231.6 7.5 %weight_grad.5 = bf16[4,4,128,1024]{3,2,1,0:T(8,128)(2,1)} custom-call(bf16[768,4096]{1,0:T(8,128)(2,1)} %get-tuple-element.212.left_ref, bf16[768,1024]{1,0:T(8,128)(2,1)} %get-tuple-element.198.right_ref), custom_call_target="tpu_custom_call" | custom-call | flops 3221225472 | bytes 14680064 | tf_op jit(solution)/shard_map/weight_grad/pallas_call | solution.py:517
  240.9 3.5 collective-permute-done.34
  254.1 3.9 collective-permute-done.38
  259.9 18.1 %weight_grad.6 = bf16[4,4,128,1024]{3,2,1,0:T(8,128)(2,1)} custom-call(bf16[768,4096]{1,0:T(8,128)(2,1)} %get-tuple-element.210.left_ref, bf16[768,1024]{1,0:T(8,128)(2,1)} %get-tuple-element.194.right_ref, bf16[4,4,128,1024]{3,2,1,0:T(8,128)(2,1)} %bitcast.50.refs_0_), custom_call_target="tpu_custom_call", output_to_operand_aliasing={{}: (2, {})} | custom-call | flops 3221225472 | bytes 14680064 | tf_op jit(solution)/shard_map/weight_grad/pallas_call | solution.py:517
  281.1 8.3 %weight_grad.7 = bf16[4,4,128,1024]{3,2,1,0:T(8,128)(2,1)} custom-call(bf16[768,4096]{1,0:T(8,128)(2,1)} %get-tuple-element.212.left_ref, bf16[768,1024]{1,0:T(8,128)(2,1)} %get-tuple-element.198.right_ref, bf16[4,4,128,1024]{3,2,1,0:T(8,128)(2,1)} %bitcast.44.refs_0_), custom_call_target="tpu_custom_call", output_to_operand_aliasing={{}: (2, {})} | custom-call | flops 3221225472 | bytes 14680064 | tf_op jit(solution)/shard_map/weight_grad/pallas_call | solution.py:517
  298.4 23.5 %attend_back.2 = (bf16[6,4,512,512]{3,2,1,0:T(8,128)(2,1)}, f32[2,400,1024]{2,1,0:T(8,128)}, bf16[3,128,1024]{2,1,0:T(8,128)(2,1)}, bf16[3,128,1024]{2,1,0:T(8,1...) custom-call(s32[1]{0:T(128)} %bitcast.me_ref, bf16[3,128,256]{2,1,0:T(8,128)(2,1)} %bitcast.138, ...), custom_call_target="tpu_custom_call" | custom-call | flops 6845104128 | bytes 22020096 | tf_op jit(solution)/shard_map/attend_back/pallas_call | solution.py:242
  327.4 24.3 %attend_back.3 = (bf16[6,4,512,512]{3,2,1,0:T(8,128)(2,1)}, f32[2,400,1024]{2,1,0:T(8,128)}, bf16[3,128,1024]{2,1,0:T(8,128)(2,1)}, bf16[3,128,1024]{2,1,0:T(8,1...) custom-call(s32[1]{0:T(128)} %bitcast.me_ref, ...), custom_call_target="tpu_custom_call", output_to_operand_aliasing={{0}: (13, {})} | custom-call | flops 6845104128 | bytes 22020096 | tf_op jit(solution)/shard_map/attend_back/pallas_call | solution.py:242
  362.4 7.1 %reduce-scatter.2.cloned.1.call-done = bf16[4,128,1024]{2,1,0:T(8,128)(2,1)} async-done(((bf16[16,128,1024]{2,1,0:T(8,128)(2,1)}), bf16[4,128,1024]{2,1,0:T(8,128)(2,1)}) %reduce-scatter.2.cloned.1.call-update) | async-done | bytes 1048592 | tf_op jit(solution)/shard_map/reduce_scatter | solution.py:856
  375.1 15.1 %collective-permute-done.51 = bf16[3,128,1024]{2,1,0:T(8,128)(2,1)} collective-permute-done((bf16[3,128,1024]{2,1,0:T(8,128)(2,1)}, bf16[3,128,1024]{2,1,0:T(8,128)(2,1)}, u32[]{:S(2)}, u32[]{:S(2)}) %collective-permute-start.51) | collective-permute-done | bytes 786464 | tf_op jit(solution)/shard_map/ppermute | solution.py:586
  390.2 16.9 %collective-permute-done.52 = bf16[3,128,1024]{2,1,0:T(8,128)(2,1)} collective-permute-done((bf16[3,128,1024]{2,1,0:T(8,128)(2,1)}, bf16[3,128,1024]{2,1,0:T(8,128)(2,1)}, u32[]{:S(2)}, u32[]{:S(2)}) %collective-permute-start.52) | collective-permute-done | bytes 786464 | tf_op jit(solution)/shard_map/ppermute | solution.py:586
  425.1 8.3 %collective-permute-done.61 = bf16[128,1024]{1,0:T(8,128)(2,1)S(1)} collective-permute-done((bf16[128,1024]{1,0:T(8,128)(2,1)S(1)}, bf16[128,1024]{1,0:T(8,128)(2,1)S(1)}, u32[]{:S(2)}, u32[]{:S(2)}) %collective-permute-start.61) | collective-permute-done | bytes 262176 | tf_op jit(solution)/shard_map/ppermute | solution.py:586
  433.4 6.4 %collective-permute-done.62 = bf16[128,1024]{1,0:T(8,128)(2,1)S(1)} collective-permute-done((bf16[128,1024]{1,0:T(8,128)(2,1)S(1)}, bf16[128,1024]{1,0:T(8,128)(2,1)S(1)}, u32[]{:S(2)}, u32[]{:S(2)}) %collective-permute-start.62) | collective-permute-done | bytes 262176 | tf_op jit(solution)/shard_map/ppermute | solution.py:586
  450.9 4.1 turn_weights.1
  (303 shorter events, 145.8 us)
Async XLA Ops:
  7.2 45.3 %all-gather.6.cloned.1.call-start = ((), (), s32[]{:S(2)}) async-start(), calls=%async_computation.3 | async-start | bytes 1474560 | tf_op jit(solution)/shard_map/all_gather | solution.py:749
  9.0 134.0 %all-gather.4.cloned.1.call-start = ((), (), s32[]{:S(2)}) async-start(), calls=%async_computation.1 | async-start | bytes 5242880 | tf_op jit(solution)/shard_map/all_gather | solution.py:774
  14.3 38.2 %collective-permute-start = (bf16[3,128,1024]{2,1,0:T(8,128)(2,1)S(1)}, bf16[3,128,1024]{2,1,0:T(8,128)(2,1)S(1)}, u32[]{:S(2)}, u32[]{:S(2)}) collective-permute-start(bf16[3,128,1024]{2,1,0:T(8,128)(2,1)S(1)} %get-tuple-element.147.refs_0_), channel_id=1, source_target_pairs={{0,8},{1,9},{2,10},{3,11},{4,12},{5,13},{6,14},{7,15},{8,0},{9,1},... | collective-permute-start | bytes 2359304 | tf_op jit(solution)/shard_map/ppermute | solution.py:586
  15.9 36.6 %collective-permute-start.1 = (bf16[3,128,1024]{2,1,0:T(8,128)(2,1)S(1)}, bf16[3,128,1024]{2,1,0:T(8,128)(2,1)}, u32[]{:S(2)}, u32[]{:S(2)}) collective-permute-start(bf16[3,128,1024]{2,1,0:T(8,128)(2,1)S(1)} %get-tuple-element.147.refs_0_), channel_id=1, source_target_pairs={{0,16},{1,17},{2,18},{3,19},{4,20},{5,21},{6,22},{7,23},{8,24},{9,... | collective-permute-start | bytes 2359304 | tf_op jit(solution)/shard_map/ppermute | solution.py:586
  16.5 29.7 %collective-permute-start.6 = (bf16[256,1024]{1,0:T(8,128)(2,1)}, bf16[256,1024]{1,0:T(8,128)(2,1)}, u32[]{:S(2)}, u32[]{:S(2)}) collective-permute-start(bf16[256,1024]{1,0:T(8,128)(2,1)} %pad_maximum_fusion.6), channel_id=1, source_target_pairs={{0,8},{1,9},{2,10},{3,11},{4,12},{5,13},{6,14},{7,15},{8,0},{9,1},... | collective-permute-start | bytes 1572872 | tf_op jit(solution)/shard_map/ppermute | solution.py:586
  52.6 316.9 %reduce-scatter.2.cloned.1.call-start = ((), (), s32[]{:S(2)}) async-start(), calls=%async_computation.2 | async-start | bytes 5242880 | tf_op jit(solution)/shard_map/reduce_scatter | solution.py:856
  52.6 30.5 %collective-permute-start.4 = (bf16[3,128,1024]{2,1,0:T(8,128)(2,1)S(1)}, bf16[3,128,1024]{2,1,0:T(8,128)(2,1)S(1)}, u32[]{:S(2)}, u32[]{:S(2)}) collective-permute-start(bf16[3,128,1024]{2,1,0:T(8,128)(2,1)S(1)} %get-tuple-element.144.refs_0_), channel_id=1, source_target_pairs={{0,8},{1,9},{2,10},{3,11},{4,12},{5,13},{6,14},{7,15},{8,0},{9,1},... | collective-permute-start | bytes 2359304 | tf_op jit(solution)/shard_map/ppermute | solution.py:586
  54.2 28.9 %collective-permute-start.5 = (bf16[3,128,1024]{2,1,0:T(8,128)(2,1)S(1)}, bf16[3,128,1024]{2,1,0:T(8,128)(2,1)S(1)}, u32[]{:S(2)}, u32[]{:S(2)}) collective-permute-start(bf16[3,128,1024]{2,1,0:T(8,128)(2,1)S(1)} %get-tuple-element.144.refs_0_), channel_id=1, source_target_pairs={{0,16},{1,17},{2,18},{3,19},{4,20},{5,21},{6,22},{7,23},{8,24},{9,... | collective-permute-start | bytes 2359304 | tf_op jit(solution)/shard_map/ppermute | solution.py:586
  56.7 26.4 %collective-permute-start.3 = (bf16[3,64,1024]{2,1,0:T(8,128)(2,1)S(1)}, bf16[3,64,1024]{2,1,0:T(8,128)(2,1)S(1)}, u32[]{:S(2)}, u32[]{:S(2)}) collective-permute-start(bf16[3,64,1024]{2,1,0:T(8,128)(2,1)S(1)} %slice.193), channel_id=1, source_target_pairs={{0,16},{1,17},{2,18},{3,19},{4,20},{5,21},{6,22},{7,23},{8,24},{9,... | collective-permute-start | bytes 1179656 | tf_op jit(solution)/shard_map/ppermute | solution.py:586
  57.9 28.2 %collective-permute-start.7 = (bf16[128,1024]{1,0:T(8,128)(2,1)S(1)}, bf16[128,1024]{1,0:T(8,128)(2,1)S(1)}, u32[]{:S(2)}, u32[]{:S(2)}) collective-permute-start(bf16[128,1024]{1,0:T(8,128)(2,1)S(1)} %copy-done.28), channel_id=1, source_target_pairs={{0,16},{1,17},{2,18},{3,19},{4,20},{5,21},{6,22},{7,23},{8,24},{9,... | collective-permute-start | bytes 786440 | tf_op jit(solution)/shard_map/ppermute | solution.py:586
  86.0 29.2 %collective-permute-start.10 = (bf16[4,144,1024]{2,1,0:T(8,128)(2,1)}, bf16[4,144,1024]{2,1,0:T(8,128)(2,1)}, u32[]{:S(2)}, u32[]{:S(2)}) collective-permute-start(bf16[4,144,1024]{2,1,0:T(8,128)(2,1)} %bitcast.13.refs_13_), channel_id=1, source_target_pairs={{0,16},{1,17},{2,18},{3,19},{4,20},{5,21},{6,22},{7,23},{8,24},{9,... | collective-permute-start | bytes 3538952 | tf_op jit(solution)/shard_map/ppermute | solution.py:586
  87.3 29.2 %collective-permute-start.9 = (bf16[4,144,1024]{2,1,0:T(8,128)(2,1)}, bf16[4,144,1024]{2,1,0:T(8,128)(2,1)}, u32[]{:S(2)}, u32[]{:S(2)}) collective-permute-start(bf16[4,144,1024]{2,1,0:T(8,128)(2,1)} %bitcast.13.refs_13_), channel_id=1, source_target_pairs={{0,8},{1,9},{2,10},{3,11},{4,12},{5,13},{6,14},{7,15},{8,0},{9,1},... | collective-permute-start | bytes 3538952 | tf_op jit(solution)/shard_map/ppermute | solution.py:586
  90.9 32.6 %collective-permute-start.11 = (bf16[3,64,1024]{2,1,0:T(8,128)(2,1)}, bf16[3,64,1024]{2,1,0:T(8,128)(2,1)S(1)}, u32[]{:S(2)}, u32[]{:S(2)}) collective-permute-start(bf16[3,64,1024]{2,1,0:T(8,128)(2,1)} %slice.197), channel_id=1, source_target_pairs={{0,16},{1,17},{2,18},{3,19},{4,20},{5,21},{6,22},{7,23},{8,24},{9,... | collective-permute-start | bytes 1179656 | tf_op jit(solution)/shard_map/ppermute | solution.py:586
  91.8 33.0 %collective-permute-start.8 = (bf16[3,64,1024]{2,1,0:T(8,128)(2,1)}, bf16[3,64,1024]{2,1,0:T(8,128)(2,1)S(1)}, u32[]{:S(2)}, u32[]{:S(2)}) collective-permute-start(bf16[3,64,1024]{2,1,0:T(8,128)(2,1)} %slice.196), channel_id=1, source_target_pairs={{0,8},{1,9},{2,10},{3,11},{4,12},{5,13},{6,14},{7,15},{8,0},{9,1},... | collective-permute-start | bytes 1179656 | tf_op jit(solution)/shard_map/ppermute | solution.py:586
  251.7 29.3 %collective-permute-start.40 = (bf16[128,1024]{1,0:T(8,128)(2,1)S(1)}, bf16[128,1024]{1,0:T(8,128)(2,1)S(1)}, u32[]{:S(2)}, u32[]{:S(2)}) collective-permute-start(bf16[128,1024]{1,0:T(8,128)(2,1)S(1)} %get-tuple-element.292), channel_id=1, source_target_pairs={{0,8},{1,9},{2,10},{3,11},{4,12},{5,13},{6,14},{7,15},{8,0},{9,1},... | collective-permute-start | bytes 786440 | tf_op jit(solution)/shard_map/ppermute | solution.py:586
  253.1 27.9 %collective-permute-start.41 = (bf16[128,1024]{1,0:T(8,128)(2,1)S(1)}, bf16[128,1024]{1,0:T(8,128)(2,1)S(1)}, u32[]{:S(2)}, u32[]{:S(2)}) collective-permute-start(bf16[128,1024]{1,0:T(8,128)(2,1)S(1)} %get-tuple-element.291), channel_id=1, source_target_pairs={{0,16},{1,17},{2,18},{3,19},{4,20},{5,21},{6,22},{7,23},{8,24},{9,... | collective-permute-start | bytes 786440 | tf_op jit(solution)/shard_map/ppermute | solution.py:586
  291.8 152.0 %all-reduce.5.cloned.1.call-start = ((), (), s32[]{:S(2)}) async-start(), calls=%async_computation.4 | async-start | bytes 2162688 | tf_op jit(solution)/shard_map/psum | solution.py:897
  295.4 26.5 %collective-permute-start.46 = (bf16[4,128,1024]{2,1,0:T(8,128)(2,1)S(1)}, bf16[4,128,1024]{2,1,0:T(8,128)(2,1)S(1)}, u32[]{:S(2)}, u32[]{:S(2)}) collective-permute-start(bf16[4,128,1024]{2,1,0:T(8,128)(2,1)S(1)} %pad_maximum_fusion.5), channel_id=1, source_target_pairs={{0,16},{1,17},{2,18},{3,19},{4,20},{5,21},{6,22},{7,23},{8,24},{9,... | collective-permute-start | bytes 3145736 | tf_op jit(solution)/shard_map/ppermute | solution.py:586
  321.9 29.9 %collective-permute-start.47 = (bf16[3,128,1024]{2,1,0:T(8,128)(2,1)}, bf16[3,128,1024]{2,1,0:T(8,128)(2,1)S(1)}, u32[]{:S(2)}, u32[]{:S(2)}) collective-permute-start(bf16[3,128,1024]{2,1,0:T(8,128)(2,1)} %get-tuple-element.230), channel_id=1, source_target_pairs={{0,8},{1,9},{2,10},{3,11},{4,12},{5,13},{6,14},{7,15},{8,0},{9,1},... | collective-permute-start | bytes 2359304 | tf_op jit(solution)/shard_map/ppermute | solution.py:586
  322.9 28.9 %collective-permute-start.48 = (bf16[3,128,1024]{2,1,0:T(8,128)(2,1)}, bf16[3,128,1024]{2,1,0:T(8,128)(2,1)S(1)}, u32[]{:S(2)}, u32[]{:S(2)}) collective-permute-start(bf16[3,128,1024]{2,1,0:T(8,128)(2,1)} %get-tuple-element.231), channel_id=1, source_target_pairs={{0,16},{1,17},{2,18},{3,19},{4,20},{5,21},{6,22},{7,23},{8,24},{9,... | collective-permute-start | bytes 2359304 | tf_op jit(solution)/shard_map/ppermute | solution.py:586
  323.9 31.1 %collective-permute-start.49 = (bf16[3,128,1024]{2,1,0:T(8,128)(2,1)}, bf16[3,128,1024]{2,1,0:T(8,128)(2,1)S(1)}, u32[]{:S(2)}, u32[]{:S(2)}) collective-permute-start(bf16[3,128,1024]{2,1,0:T(8,128)(2,1)} %get-tuple-element.232), channel_id=1, source_target_pairs={{0,24},{1,25},{2,26},{3,27},{4,28},{5,29},{6,30},{7,31},{8,16},{9,... | collective-permute-start | bytes 2359304 | tf_op jit(solution)/shard_map/ppermute | solution.py:586
  371.0 36.2 %collective-permute-start.52 = (bf16[3,128,1024]{2,1,0:T(8,128)(2,1)}, bf16[3,128,1024]{2,1,0:T(8,128)(2,1)}, u32[]{:S(2)}, u32[]{:S(2)}) collective-permute-start(bf16[3,128,1024]{2,1,0:T(8,128)(2,1)} %get-tuple-element.255), channel_id=1, source_target_pairs={{0,16},{1,17},{2,18},{3,19},{4,20},{5,21},{6,22},{7,23},{8,24},{9,... | collective-permute-start | bytes 2359304 | tf_op jit(solution)/shard_map/ppermute | solution.py:586
  372.4 41.9 %collective-permute-start.53 = (bf16[3,128,1024]{2,1,0:T(8,128)(2,1)}, bf16[3,128,1024]{2,1,0:T(8,128)(2,1)}, u32[]{:S(2)}, u32[]{:S(2)}) collective-permute-start(bf16[3,128,1024]{2,1,0:T(8,128)(2,1)} %get-tuple-element.256), channel_id=1, source_target_pairs={{0,24},{1,25},{2,26},{3,27},{4,28},{5,29},{6,30},{7,31},{8,16},{9,... | collective-permute-start | bytes 2359304 | tf_op jit(solution)/shard_map/ppermute | solution.py:586
  413.3 26.5 %collective-permute-start.62 = (bf16[128,1024]{1,0:T(8,128)(2,1)S(1)}, bf16[128,1024]{1,0:T(8,128)(2,1)S(1)}, u32[]{:S(2)}, u32[]{:S(2)}) collective-permute-start(bf16[128,1024]{1,0:T(8,128)(2,1)S(1)} %get-tuple-element.282), channel_id=1, source_target_pairs={{0,6},{1,7},{2,4},{3,5},{4,2},{5,3},{6,0},{7,1},{8,14},{9,15},{10,... | collective-permute-start | bytes 786440 | tf_op jit(solution)/shard_map/ppermute | solution.py:586
  (98 other events, 1170.7 us)
Sparse Core Ops, SparseCore 0:
  10.2 33.1 all-gather.5
  52.7 81.3 all-gather.3
  291.9 77.5 reduce-scatter.1
  375.2 68.5 all-reduce.4
